TPU v7x, 32 devices: a whole 2x2x4 slice. The times are simulated.
32 devices in a mesh: groups: 2 (over y), tile: 4 (over z), chan: 2 (over x), sub: 2 (over core).
Axes of the slice: x: 2, y: 2, z: 4, core: 2. Of those that a mesh axis runs over, the one named last changes fastest.
Arguments:
- canvas: bfloat16 [64, 64, 1280], P(('groups', 'tile'), 'sub'), parts along dimension 0, may hold values from -300 to 300
- thumb: bfloat16 [512, 1280], P(('groups', 'tile')), parts along dimension 0, may hold values from -18 to 18
- ramps: int32 [4, 16], replicated, may hold values from 1 to 8
- t_embed: float32 [5120], P('groups'), parts along dimension 0, may hold values from -3 to 3
- norm_gain: float32 [1280], replicated, may hold values from 0.1 to 1.9
- w_query: bfloat16 [1280, 1280], P(None, 'chan'), may hold values from -0.15625 to 0.15625
- w_key: bfloat16 [1280, 1280], P(None, 'chan'), may hold values from -0.15625 to 0.15625
- w_value: bfloat16 [1280, 1280], P(None, 'chan'), may hold values from -0.15625 to 0.15625
- w_out: bfloat16 [1280, 1280], P('chan'), may hold values from -0.375 to 0.375
Outputs:
- blended: bfloat16 [64, 64, 1280], P(('groups', 'tile'), 'sub', 'chan'), parts along dimension 0
There are 2 independent parts, one for each index of `groups`. A program takes and returns all parts, laid end to end along the dimension named above; an argument that names none is the same for every part. Nothing has to cross between parts.
All inputs are finite; a program needn't handle non-finite values.
Results may differ from a plain program's by a relative error of at most 0.012.
The roundings to bfloat16 on the way count: a program that leaves them out, or rounds other values in their place, can miss the bound.
Values may be sent and summed in bfloat16 or wider, within the bound.
No kernel may reach another device: no remote copies, remote signals or barrier semaphores. Data moves between devices by JAX's collectives and lax.ppermute only.
A program may use at most 128 MiB of HBM per device.

v0:
```python
import jax
import jax.numpy as jnp
from jax import lax
from jax.sharding import PartitionSpec as P

HD = 64
GROUPS = 32
M = 4


def extended_2(x, sides, width):
    for axis, dim in sides:
        peers, length = (lax.axis_size(axis), x.shape[dim])
        up = [(i, (i + 1) % peers) for i in range(peers - 1)]
        down = [(j, i) for i, j in up]
        last = lax.slice_in_dim(x, length - width, length, axis=dim)
        initial = lax.slice_in_dim(x, 0, width, axis=dim)
        before = lax.ppermute(last, axis, up)
        after = lax.ppermute(initial, axis, down)
        x = jnp.concatenate([before, x, after], axis=dim)
    return x


def from_behind(value, axis, steps):
    count = lax.axis_size(axis)
    initial, last = (max(0, -steps), min(count, count - steps))
    return lax.ppermute(value, axis, [(source, source + steps) for source in range(initial, last)])


def on_device(canvas, thumb, ramps, t_embed, norm_gain, w_query, w_key, w_value, w_out):
    owned = canvas.shape[0]
    columns = canvas.shape[1]
    channels = canvas.shape[2]
    rows_tile = owned + 2 * M
    tokens = rows_tile * columns
    local_ch = w_query.shape[1]
    heads_here = local_ch // HD
    group_ch = channels // GROUPS
    extended = extended_2(canvas, (("tile", 0),), M)
    grouped = extended.astype(jnp.float32).reshape(rows_tile, columns, GROUPS, group_ch)
    count = rows_tile * columns * lax.axis_size("sub") * group_ch
    sums = lax.psum(jnp.sum(grouped, axis=(0, 1, 3)), "sub")
    mean = sums / count
    centered = grouped - mean[None, None, :, None]
    squares = lax.psum(jnp.sum(centered * centered, axis=(0, 1, 3)), "sub")
    var = squares / count
    scale = t_embed[:channels]
    shift = t_embed[channels:]
    normed = (centered / jnp.sqrt(var + 1e-05)[None, None, :, None]).reshape(
        rows_tile, columns, channels
    )
    normed = (normed * norm_gain * (1.0 + scale) + shift).astype(jnp.bfloat16)
    query = jnp.dot(
        normed.reshape(tokens, channels), w_query, preferred_element_type=jnp.float32
    ).astype(jnp.bfloat16)
    query3 = query.reshape(tokens, heads_here, HD)
    piece = lax.all_gather(thumb, "tile", axis=0, tiled=True)
    keys = jnp.dot(piece, w_key, preferred_element_type=jnp.float32).astype(jnp.bfloat16)
    values = jnp.dot(piece, w_value, preferred_element_type=jnp.float32).astype(jnp.bfloat16)
    top = jnp.full((heads_here, tokens), -1e30, jnp.float32)
    count_keys = keys.shape[0]
    keys3 = keys.reshape(count_keys, heads_here, HD)
    values3 = values.reshape(count_keys, heads_here, HD)
    scores = jnp.einsum("qhd,khd->hqk", query3, keys3, preferred_element_type=jnp.float32) * 0.125
    new_top = jnp.maximum(top, jnp.max(scores, axis=-1))
    expo = jnp.exp(scores - new_top[:, :, None])
    total = jnp.sum(expo, axis=-1)
    added = jnp.einsum(
        "hqk,khd->qhd", expo.astype(jnp.bfloat16), values3, preferred_element_type=jnp.float32
    )
    accum = added
    top, total, accum = (new_top, total, accum)
    attended = (
        (accum / jnp.transpose(total)[:, :, None]).astype(jnp.bfloat16).reshape(tokens, local_ch)
    )
    term = jnp.dot(attended, w_out, preferred_element_type=jnp.float32)
    pred = lax.psum_scatter(
        term.astype(jnp.bfloat16), "chan", scatter_dimension=1, tiled=True
    ).astype(jnp.float32)
    out_ch = pred.shape[1]
    pred = pred.reshape(rows_tile, columns, out_ch)
    tile_pos = lax.axis_index("tile")
    tile_count = lax.axis_size("tile")
    ramp_own = lax.dynamic_slice_in_dim(ramps, tile_pos, 1, 0)[0].astype(jnp.float32)
    above_pos = jnp.maximum(tile_pos - 1, 0)
    below_pos = jnp.minimum(tile_pos + 1, tile_count - 1)
    ramp_above = lax.dynamic_slice_in_dim(ramps, above_pos, 1, 0)[0].astype(jnp.float32)
    ramp_below = lax.dynamic_slice_in_dim(ramps, below_pos, 1, 0)[0].astype(jnp.float32)
    ramp_above = jnp.where(tile_pos > 0, ramp_above, 0.0)
    ramp_below = jnp.where(tile_pos < tile_count - 1, ramp_below, 0.0)
    weighted = pred * ramp_own[:, None, None]
    from_above = from_behind(weighted[M + owned :].astype(jnp.bfloat16), "tile", 1).astype(
        jnp.float32
    )
    from_below = from_behind(weighted[:M].astype(jnp.bfloat16), "tile", -1).astype(jnp.float32)
    numer = weighted[M : M + owned].at[:M].add(from_above).at[owned - M :].add(from_below)
    denom = (
        ramp_own[M : M + owned]
        .at[:M]
        .add(ramp_above[M + owned :])
        .at[owned - M :]
        .add(ramp_below[:M])
    )
    return (numer / denom[:, None, None]).astype(jnp.bfloat16)


def solution(mesh):
    placed = (
        P(("groups", "tile"), "sub", None),
        P(("groups", "tile"), None),
        P(),
        P("groups"),
        P(),
        P(None, "chan"),
        P(None, "chan"),
        P(None, "chan"),
        P("chan", None),
    )
    return jax.shard_map(
        on_device,
        mesh=mesh,
        in_specs=placed,
        out_specs=P(("groups", "tile"), "sub", "chan"),
        check_vma=False,
    )
```

profile of v0, /device:TPU:0, one launch (start us, length us, event | category | flops | bytes accessed | tf_op | source)
XLA Modules:
  0.0 118.6 jit_solution(4736441093196080622)
XLA Ops:
  6.5 2.0 %fusion.27 = (bf16[4,32,1280]{2,1,0:T(8,128)(2,1)}, bf16[4,32,1280]{2,1,0:T(8,128)(2,1)S(1)}) fusion(bf16[8,32,1280]{2,1,0:T(8,128)(2,1)} %param.17), kind=kLoop, calls=%fused_computation.50 | loop fusion | bytes 1310720 | tf_op jit(solution)/shard_map/slice | solution.py:16
  8.6 5.7 %collective-permute-start = (bf16[4,32,1280]{2,1,0:T(8,128)(2,1)}, bf16[4,32,1280]{2,1,0:T(8,128)(2,1)}, u32[]{:S(2)}, u32[]{:S(2)}) collective-permute-start(bf16[4,32,1280]{2,1,0:T(8,128)(2,1)} %get-tuple-element.57), channel_id=1, source_target_pairs={{0,4},{4,8},{8,12},{1,5},{5,9},{9,13},{2,6},{6,10},{10,14},{3,7},{... | collective-permute-start | bytes 983048 | tf_op jit(solution)/shard_map/ppermute | solution.py:18
  14.2 1.3 %collective-permute-start.1 = (bf16[4,32,1280]{2,1,0:T(8,128)(2,1)S(1)}, bf16[4,32,1280]{2,1,0:T(8,128)(2,1)}, u32[]{:S(2)}, u32[]{:S(2)}) collective-permute-start(bf16[4,32,1280]{2,1,0:T(8,128)(2,1)S(1)} %get-tuple-element.58), channel_id=1, source_target_pairs={{4,0},{8,4},{12,8},{5,1},{9,5},{13,9},{6,2},{10,6},{14,10},{7,3},{... | collective-permute-start | bytes 983048 | tf_op jit(solution)/shard_map/ppermute | solution.py:19
  15.5 23.5 %all_gather.3 = bf16[256,1280]{1,0:T(8,128)(2,1)S(1)} all-gather(bf16[64,1280]{1,0:T(8,128)(2,1)} %param.18), channel_id=1, replica_groups=mesh['groups'=2,'tile'=4,'chan'=2,'sub'=2] {'tile'}, dimensions={0}, use_global_device_ids=true | all-gather | bytes 819200 | tf_op jit(solution)/shard_map/all_gather | solution.py:57
  39.0 2.2 %convolution_convert_fusion.2 = bf16[256,640]{1,0:T(8,128)(2,1)S(1)} fusion(bf16[256,1280]{1,0:T(8,128)(2,1)S(1)} %all_gather.3, bf16[1280,640]{1,0:T(8,128)(2,1)} %param.23), kind=kOutput, calls=%fused_computation.24 | convolution fusion | flops 419594240 | bytes 2621440 | tf_op jit(solution)/shard_map/dot_general | solution.py:58
  41.2 0.7 convolution_convert_fusion.3
  41.9 0.0 copy-start.4
  41.9 4.9 %concatenate.23 = bf16[8,32,32,40]{3,2,1,0:T(8,128)(2,1)} reshape(bf16[8,32,1280]{2,1,0:T(8,128)(2,1)S(1)} %copy-done.1) | data formatting | bytes 1310720 | tf_op jit(solution)/shard_map/concatenate | solution.py:20
  46.8 0.9 copy.18
  47.7 0.9 copy.20
  48.6 0.0 collective-permute-done.1
  48.6 2.9 %concatenate.24 = bf16[4,32,32,40]{3,2,1,0:T(8,128)(2,1)S(1)} reshape(bf16[4,32,1280]{2,1,0:T(8,128)(2,1)} %collective-permute-done.1) | data formatting | bytes 655360 | tf_op jit(solution)/shard_map/concatenate | solution.py:20
  51.5 0.0 collective-permute-done
  51.5 3.6 %concatenate.22 = bf16[4,32,32,40]{3,2,1,0:T(8,128)(2,1)} reshape(bf16[4,32,1280]{2,1,0:T(8,128)(2,1)} %collective-permute-done) | data formatting | bytes 655360 | tf_op jit(solution)/shard_map/concatenate | solution.py:20
  55.1 2.7 %convert_reduce_fusion = f32[32]{0:T(128)S(1)} fusion(bf16[4,32,32,40]{3,2,1,0:T(8,128)(2,1)S(1)} %concatenate.24, bf16[8,32,32,40]{3,2,1,0:T(8,128)(2,1)} %concatenate.23, bf16[4,32,32,40]{3,2,1,0:T(8,128)(2,1)} %concatenate.22), kind=kLoop, calls=%fused_computation.1 | loop fusion | flops 2621408 | bytes 1310848 | tf_op jit(solution)/shard_map/reduce_sum | solution.py:42
  57.7 2.5 %psum.14 = f32[32]{0:T(128)S(1)} all-reduce(f32[32]{0:T(128)S(1)} %convert_reduce_fusion), channel_id=1, replica_groups=mesh['groups'=2,'tile'=4,'chan'=2,'sub'=2] {'sub'}, use_global_device_ids=true, to_apply=%region_1.0 | all-reduce | flops 32 | bytes 256 | tf_op jit(solution)/shard_map/psum | solution.py:42
  60.2 3.4 %fusion.1 = f32[32]{0:T(128)S(1)} fusion(f32[32]{0:T(128)S(1)} %broadcast_multiply_fusion, bf16[4,32,32,40]{3,2,1,0:T(8,128)(2,1)S(1)} %concatenate.24, bf16[8,32,32,40]{3,2,1,0:T(8,128)(2,1)} %concatenate.23, bf16[4,32,32,40]{3,2,1,0:T(8,128)(2,1)} %concatenate.22), kind=kLoop, calls=%fused_computation.3 | loop fusion | flops 3932128 | bytes 1310976 | tf_op jit(solution)/shard_map/reduce_sum | solution.py:45
  63.6 2.6 %psum.15 = f32[32]{0:T(128)S(1)} all-reduce(f32[32]{0:T(128)S(1)} %fusion.1), channel_id=1, replica_groups=mesh['groups'=2,'tile'=4,'chan'=2,'sub'=2] {'sub'}, use_global_device_ids=true, to_apply=%region_3.0 | all-reduce | flops 32 | bytes 256 | tf_op jit(solution)/shard_map/psum | solution.py:45
  66.3 0.1 div.38
  66.3 0.1 div.39
  66.4 0.1 sub.29
  66.5 0.1 sub.30
  66.6 0.0 copy-start.8
  66.6 1.3 %pad_maximum_fusion.1 = bf16[16,32,1280]{2,1,0:T(8,128)(2,1)S(1)} fusion(bf16[4,32,1280]{2,1,0:T(8,128)(2,1)} %collective-permute-done.1, bf16[8,32,1280]{2,1,0:T(8,128)(2,1)S(1)} %copy-done.1, bf16[4,32,1280]{2,1,0:T(8,128)(2,1)} %collective-permute-done), kind=kLoop, calls=%fused_computation.21 | loop fusion | flops 1310720 | bytes 2621440 | tf_op jit(solution)/shard_map/concatenate | solution.py:20
  68.0 0.7 fusion.10
  68.6 1.2 %convolution_convert_fusion.1 = bf16[512,640]{1,0:T(8,128)(2,1)S(1)} fusion(bf16[512,1280]{1,0:T(8,128)(2,1)S(1)} %fusion.10, bf16[1280,640]{1,0:T(8,128)(2,1)S(1)} %copy-done.8), kind=kOutput, calls=%fused_computation.20 | convolution fusion | flops 839188480 | bytes 3604480 | tf_op jit(solution)/shard_map/dot_general | solution.py:53
  69.8 0.3 copy.19
  70.1 0.9 multiply_reduce_fusion
  71.0 0.0 copy-start.3
  71.0 0.9 fusion.2
  71.9 0.1 copy-done.3
  72.0 1.1 divide_convert_fusion
  73.1 1.2 %convolution_convert_fusion = bf16[512,1280]{1,0:T(8,128)(2,1)S(1)} fusion(bf16[512,640]{0,1:T(8,128)(2,1)S(1)} %bitcast.44, bf16[640,1280]{1,0:T(8,128)(2,1)S(1)} %copy-done), kind=kOutput, calls=%fused_computation.9 | convolution fusion | flops 839516160 | bytes 3604480 | tf_op jit(solution)/shard_map/dot_general | solution.py:76
  74.3 0.0 copy-start.6
  74.3 1.5 %copy.23 = bf16[512,1280]{0,1:T(8,128)(2,1)} copy(bf16[512,1280]{1,0:T(8,128)(2,1)S(1)} %convolution_convert_fusion) | data formatting | bytes 2621440
  75.8 0.0 reduce-scatter.4.cloned.1.call-update
  75.9 0.1 slice_bitcast_fusion
  76.0 0.1 constant_dynamic-update-slice_fusion
  76.0 22.2 %reduce-scatter.4.cloned.1.call-done = bf16[640,512]{1,0:T(8,128)(2,1)} async-done(((bf16[1280,512]{1,0:T(8,128)(2,1)}), bf16[640,512]{1,0:T(8,128)(2,1)}) %reduce-scatter.4.cloned.1.call-update) | async-done | bytes 655376
  98.3 1.4 %copy.24 = bf16[512,640]{1,0:T(8,128)(2,1)S(1)} copy(bf16[512,640]{0,1:T(8,128)(2,1)} %bitcast.41) | data formatting | bytes 1310720
  99.7 0.2 fusion.25
  99.9 3.4 %collective-permute-start.2 = (bf16[4,32,640]{2,1,0:T(8,128)(2,1)S(1)}, bf16[4,32,640]{2,1,0:T(8,128)(2,1)S(1)}, u32[]{:S(2)}, u32[]{:S(2)}) collective-permute-start(bf16[4,32,640]{2,1,0:T(8,128)(2,1)S(1)} %get-tuple-element.56), channel_id=1, source_target_pairs={{0,4},{4,8},{8,12},{1,5},{5,9},{9,13},{2,6},{6,10},{10,14},{3,7},{... | collective-permute-start | bytes 491528 | tf_op jit(solution)/shard_map/ppermute | solution.py:27
  103.3 0.1 fusion.23
  103.5 1.3 %collective-permute-start.3 = (bf16[4,32,640]{2,1,0:T(8,128)(2,1)S(1)}, bf16[4,32,640]{2,1,0:T(8,128)(2,1)S(1)}, u32[]{:S(2)}, u32[]{:S(2)}) collective-permute-start(bf16[4,32,640]{2,1,0:T(8,128)(2,1)S(1)} %get-tuple-element.55), channel_id=1, source_target_pairs={{4,0},{8,4},{12,8},{5,1},{9,5},{13,9},{6,2},{10,6},{14,10},{7,3},{... | collective-permute-start | bytes 491528 | tf_op jit(solution)/shard_map/ppermute | solution.py:27
  104.8 1.8 %collective-permute-done.2 = bf16[4,32,640]{2,1,0:T(8,128)(2,1)S(1)} collective-permute-done((bf16[4,32,640]{2,1,0:T(8,128)(2,1)S(1)}, bf16[4,32,640]{2,1,0:T(8,128)(2,1)S(1)}, u32[]{:S(2)}, u32[]{:S(2)}) %collective-permute-start.2) | collective-permute-done | bytes 163872 | tf_op jit(solution)/shard_map/ppermute | solution.py:27
  106.6 4.2 %collective-permute-done.3 = bf16[4,32,640]{2,1,0:T(8,128)(2,1)S(1)} collective-permute-done((bf16[4,32,640]{2,1,0:T(8,128)(2,1)S(1)}, bf16[4,32,640]{2,1,0:T(8,128)(2,1)S(1)}, u32[]{:S(2)}, u32[]{:S(2)}) %collective-permute-start.3) | collective-permute-done | bytes 163872 | tf_op jit(solution)/shard_map/ppermute | solution.py:27
  110.8 0.1 fusion.18
  110.9 0.8 divide_convert_fusion.1
  (24 shorter events, 0.2 us)
Async XLA Ops:
  6.5 66.5 %copy-start = (bf16[640,1280]{1,0:T(8,128)(2,1)S(1)}, bf16[640,1280]{1,0:T(8,128)(2,1)}, u32[]{:S(2)}) copy-start(bf16[640,1280]{1,0:T(8,128)(2,1)} %param.25) | copy-start | bytes 4915204
  6.5 91.7 %reduce-scatter.4.cloned.1.call-start = ((), (), s32[]{:S(2)}) async-start(), calls=%async_computation.1 | async-start | bytes 1966080
  6.5 34.7 %copy-start.7 = (bf16[1280,640]{1,0:T(8,128)(2,1)S(1)}, bf16[1280,640]{1,0:T(8,128)(2,1)}, u32[]{:S(2)}) copy-start(bf16[1280,640]{1,0:T(8,128)(2,1)} %param.24) | copy-start | bytes 4915204
  8.6 42.9 %collective-permute-start = (bf16[4,32,1280]{2,1,0:T(8,128)(2,1)}, bf16[4,32,1280]{2,1,0:T(8,128)(2,1)}, u32[]{:S(2)}, u32[]{:S(2)}) collective-permute-start(bf16[4,32,1280]{2,1,0:T(8,128)(2,1)} %get-tuple-element.57), channel_id=1, source_target_pairs={{0,4},{4,8},{8,12},{1,5},{5,9},{9,13},{2,6},{6,10},{10,14},{3,7},{... | collective-permute-start | bytes 983048 | tf_op jit(solution)/shard_map/ppermute | solution.py:18
  14.2 34.4 %collective-permute-start.1 = (bf16[4,32,1280]{2,1,0:T(8,128)(2,1)S(1)}, bf16[4,32,1280]{2,1,0:T(8,128)(2,1)}, u32[]{:S(2)}, u32[]{:S(2)}) collective-permute-start(bf16[4,32,1280]{2,1,0:T(8,128)(2,1)S(1)} %get-tuple-element.58), channel_id=1, source_target_pairs={{4,0},{8,4},{12,8},{5,1},{9,5},{13,9},{6,2},{10,6},{14,10},{7,3},{... | collective-permute-start | bytes 983048 | tf_op jit(solution)/shard_map/ppermute | solution.py:19
  39.0 2.9 %copy-start.1 = (bf16[8,32,1280]{2,1,0:T(8,128)(2,1)S(1)}, bf16[8,32,1280]{2,1,0:T(8,128)(2,1)}, u32[]{:S(2)}) copy-start(bf16[8,32,1280]{2,1,0:T(8,128)(2,1)} %param.17) | copy-start | bytes 1966084
  41.9 6.7 %copy-start.4 = (f32[2560]{0:T(1024)S(1)}, f32[2560]{0:T(1024)}, u32[]{:S(2)}) copy-start(f32[2560]{0:T(1024)} %param.20) | copy-start | bytes 30724
  60.2 7.8 %copy-start.5 = (f32[1280]{0:T(1024)S(1)}, f32[1280]{0:T(1024)}, u32[]{:S(2)}) copy-start(f32[1280]{0:T(1024)} %param.21) | copy-start | bytes 15364
  66.6 2.0 %copy-start.8 = (bf16[1280,640]{1,0:T(8,128)(2,1)S(1)}, bf16[1280,640]{1,0:T(8,128)(2,1)}, u32[]{:S(2)}) copy-start(bf16[1280,640]{1,0:T(8,128)(2,1)} %param.22) | copy-start | bytes 4915204
  68.6 1.5 %copy-start.2 = (bf16[256,640]{0,1:T(8,128)(2,1)S(1)}, bf16[256,640]{0,1:T(8,128)(2,1)}, u32[]{:S(2)}) copy-start(bf16[256,640]{0,1:T(8,128)(2,1)} %copy.20) | copy-start | bytes 983044
  71.0 1.0 copy-start.3
  74.3 1.5 %copy-start.6 = (s32[4,16]{1,0:T(4,128)S(1)}, s32[4,16]{1,0:T(4,128)}, u32[]{:S(2)}) copy-start(s32[4,16]{1,0:T(4,128)} %param.19) | copy-start | bytes 772
  99.9 6.7 %collective-permute-start.2 = (bf16[4,32,640]{2,1,0:T(8,128)(2,1)S(1)}, bf16[4,32,640]{2,1,0:T(8,128)(2,1)S(1)}, u32[]{:S(2)}, u32[]{:S(2)}) collective-permute-start(bf16[4,32,640]{2,1,0:T(8,128)(2,1)S(1)} %get-tuple-element.56), channel_id=1, source_target_pairs={{0,4},{4,8},{8,12},{1,5},{5,9},{9,13},{2,6},{6,10},{10,14},{3,7},{... | collective-permute-start | bytes 491528 | tf_op jit(solution)/shard_map/ppermute | solution.py:27
  103.5 7.4 %collective-permute-start.3 = (bf16[4,32,640]{2,1,0:T(8,128)(2,1)S(1)}, bf16[4,32,640]{2,1,0:T(8,128)(2,1)S(1)}, u32[]{:S(2)}, u32[]{:S(2)}) collective-permute-start(bf16[4,32,640]{2,1,0:T(8,128)(2,1)S(1)} %get-tuple-element.55), channel_id=1, source_target_pairs={{4,0},{8,4},{12,8},{5,1},{9,5},{13,9},{6,2},{10,6},{14,10},{7,3},{... | collective-permute-start | bytes 491528 | tf_op jit(solution)/shard_map/ppermute | solution.py:27
Sparse Core Ops, SparseCore 0:
  75.9 22.3 reduce-scatter.3
where the time goes:
time: 119 us
  blocking collectives  28.6 us (24%)
  waiting for transfers between devices  28.3 us (24%)
  local copies, waits for them, and re-layouts  18.8 us (16%)
  between operations  13.7 us (12%)
  starting transfers between devices  11.6 us (10%)
  other arithmetic  10.4 us (9%)
  matrix products  7.22 us (6%)
    all_gather x1, blocking collectives, on_device(): piece = lax.all_gather(thumb, 'tile', axis=0, tiled=True)  23.5 us
    unnamed x2, waiting for transfers between devices  22.3 us
    concatenate x3, local copies, waits for them, and re-layouts, extended_2(): x = jnp.concatenate([before, x, after], axis=dim)  11.3 us
    ppermute x2, waiting for transfers between devices, from_behind(): lax.ppermute(value, axis, [(source, source + steps) for source in range(i...  5.99 us
    ppermute x1, starting transfers between devices, extended_2(): before = lax.ppermute(last, axis, up)  5.67 us
    ppermute x2, starting transfers between devices, from_behind(): lax.ppermute(value, axis, [(source, source + steps) for source in range(i...  4.67 us
    reduce_sum x1, other arithmetic, on_device(): squares = lax.psum(jnp.sum(centered * centered, axis=(0, 1, 3)), 'sub')  3.4 us
    unnamed x20, local copies, waits for them, and re-layouts  2.98 us
  transfers between devices with their start and end apart: 5, of which 3 were waited for; matrix products, arithmetic and copies ran while one was open for 11% of the time, Pallas kernels for 0%

commit v1 on v0

v1 whole, which is shorter than its diff:
```python
import functools

import jax
import jax.numpy as jnp
from jax import lax
from jax.experimental import pallas as pl
from jax.experimental.pallas import tpu as pltpu
from jax.sharding import PartitionSpec as P

HD = 64
GROUPS = 32
M = 4
LANES = 128
EPS = 1e-05
F32 = jnp.float32
BF16 = jnp.bfloat16
NT = (((1,), (1,)), ((), ()))


def three_parts(v):
    hi = v.astype(BF16).astype(F32)
    rest = v - hi
    mid = rest.astype(BF16).astype(F32)
    return hi, mid, rest - mid


def group_of_channel(channels):
    size = channels // GROUPS
    row = lax.broadcasted_iota(jnp.int32, (LANES, channels), 0)
    col = lax.broadcasted_iota(jnp.int32, (LANES, channels), 1)
    first = row * size
    return jnp.where((col >= first) & (col < first + size), 1.0, 0.0).astype(BF16)


def exact_dot(v, member, dims):
    parts = jnp.concatenate(three_parts(v), axis=0).astype(BF16)
    out = lax.dot_general(parts, member, dims, preferred_element_type=F32)
    return out[0:8] + out[8:16] + out[16:24]


def rows_of(pairs, width):
    row = lax.broadcasted_iota(jnp.int32, (8, width), 0)
    out = jnp.zeros((8, width), F32)
    for i, v in pairs.items():
        out = jnp.where(row == i, jnp.broadcast_to(v, (8, width)), out)
    return out


def local_stats(canvas_ref, thumb_ref, pay_ref, st_ref):
    channels = canvas_ref.shape[1]
    half = pay_ref.shape[0]
    n = canvas_ref.shape[0] // 2
    size = channels // GROUPS
    sub = lax.axis_index("sub")
    start = pl.multiple_of(sub * half, half)
    pay_ref[:, :channels] = thumb_ref[pl.ds(start, half), :]
    means, squares = [], []
    for b in range(2):
        x = canvas_ref[b * n : (b + 1) * n, :].astype(F32)
        mean = jnp.sum(x, axis=0, keepdims=True) * (1.0 / n)
        c = x - mean
        means.append(mean)
        squares.append(jnp.sum(c * c, axis=0, keepdims=True))
    member = group_of_channel(channels)
    mean_g = exact_dot(rows_of({0: means[0], 1: means[1]}, channels), member, NT) * (1.0 / size)
    back = exact_dot(mean_g, member, (((1,), (0,)), ((), ())))
    tot = []
    for b in range(2):
        diff = means[b] - back[b : b + 1]
        tot.append(squares[b] + n * (diff * diff))
    m2_g = exact_dot(rows_of({2: tot[0], 3: tot[1]}, channels), member, NT)
    parts = three_parts(mean_g + m2_g)
    pad = jnp.zeros((half - 24, LANES), F32)
    block = jnp.concatenate(list(parts) + [pad], axis=0).astype(BF16)
    pay_ref[:, channels:] = block
    st_ref[...] = block


def row_weights(ramps_ref, tile, n_tile, columns, upper):
    owned = 2 * M
    shape = (M * columns, 1)
    row = lax.broadcasted_iota(jnp.int32, shape, 0)
    own = jnp.zeros(shape, F32)
    other = jnp.zeros(shape, F32)
    if upper:
        peer, live = jnp.maximum(tile - 1, 0), tile > 0
    else:
        peer, live = jnp.minimum(tile + 1, n_tile - 1), tile < n_tile - 1
    gate = jnp.where(live, 1.0, 0.0).astype(F32)
    for r in range(M):
        here = (row >= r * columns) & (row < (r + 1) * columns)
        own_r = ramps_ref[tile, (M if upper else 2 * M) + r].astype(F32)
        other_r = ramps_ref[peer, (M + owned if upper else 0) + r].astype(F32) * gate
        own = jnp.where(here, own_r, own)
        other = jnp.where(here, other_r, other)
    total = own + other
    return own / total, other / total


def attend(q, k_ref, v_ref, wo_ref, weights, bl_ref, send_ref, own_ref, split):
    n = bl_ref.shape[0]
    w_own, w_other = weights
    width = k_ref.shape[1]
    for j in range(width // LANES):
        cols = slice(j * LANES, (j + 1) * LANES)
        qp = q(cols)
        kp, vp = k_ref[:, cols], v_ref[:, cols]
        low = lax.broadcasted_iota(jnp.int32, kp.shape, 1) < HD
        zero = jnp.zeros_like(kp)
        out = None
        for h in range(2):
            keep = low if h == 0 else jnp.logical_not(low)
            k_h, v_h = jnp.where(keep, kp, zero), jnp.where(keep, vp, zero)
            s = lax.dot_general(qp, k_h, NT, preferred_element_type=F32)
            p = jnp.exp(s - jnp.max(s, axis=1, keepdims=True))
            total = jnp.sum(p, axis=1, keepdims=True)
            o = jnp.dot(p.astype(BF16), v_h, preferred_element_type=F32) * (1.0 / total)
            out = o if out is None else out + o
        att = out.astype(BF16).astype(F32)
        bl_ref[:, cols] = (att[:n] * w_own + att[n:] * w_other).astype(BF16)
    term = jnp.dot(bl_ref[...], wo_ref[...], preferred_element_type=F32)
    if split:
        half = term.shape[1] // 2
        first = lax.axis_index("chan") == 0
        lo, hi = term[:, :half], term[:, half:]
        own_ref[...] = jnp.where(first, lo, hi).astype(BF16)
        send_ref[...] = jnp.where(first, hi, lo).astype(BF16)
    else:
        send_ref[...] = term.astype(BF16)


def merged_stats(stats, tile, n_tile, count, member):
    live = {}
    for o in range(-2, 3):
        ok = (tile + o >= 0) & (tile + o < n_tile)
        gate = jnp.where(ok, 1.0, 0.0).astype(F32)
        live[o] = [v * gate for v in stats[o]]
    rows = {}
    for i, o in enumerate((-1, 0, 1)):
        blocks = []
        for s in range(len(stats[0])):
            blocks += [
                (live[o - 1][s][1:2], live[o - 1][s][3:4]),
                (live[o][s][0:1], live[o][s][2:3]),
                (live[o][s][1:2], live[o][s][3:4]),
                (live[o + 1][s][0:1], live[o + 1][s][2:3]),
            ]
        mean = sum(m for m, _ in blocks) * (1.0 / len(blocks))
        m2 = sum(q for _, q in blocks) + count * sum((m - mean) * (m - mean) for m, _ in blocks)
        rows[i] = mean
        rows[3 + i] = 1.0 / jnp.sqrt(m2 * (1.0 / (count * len(blocks))) + EPS)
    return exact_dot(rows_of(rows, LANES), member, (((1,), (0,)), ((), ())))


def fill_normed(canvas_ref, rows, affine, normed_ref, order):
    chan, gain, shift = affine
    n = normed_ref.shape[0] // 2
    x = canvas_ref[rows, :].astype(F32)
    for i, o in enumerate(order):
        mean, rstd = chan[o + 1 : o + 2], chan[o + 4 : o + 5]
        normed_ref[i * n : (i + 1) * n, :] = ((x - mean) * (rstd * gain) + shift).astype(BF16)


def first_block(n_tile, split, count, columns, *refs):
    (ramps_ref, canvas_ref, thumb_ref, temb_ref, gain_ref, wq_ref, wk_ref, wv_ref, wo_ref, st_ref, st_peer_ref) = refs[:11]
    near = refs[11 : 11 + n_tile - 1]
    far = refs[11 + n_tile - 1 : 11 + 2 * (n_tile - 1)]
    rest = refs[11 + 2 * (n_tile - 1) :]
    if split:
        send_ref, own_ref, k_ref, v_ref, chan_ref, all_ref, normed_ref, q_ref, bl_ref = rest
    else:
        send_ref, k_ref, v_ref, chan_ref, all_ref, normed_ref, q_ref, bl_ref = rest
        own_ref = None
    channels = canvas_ref.shape[1]
    half = near[0].shape[0]
    tile = lax.axis_index("tile")

    def stat(ref, lanes):
        v = ref[:, lanes].astype(F32)
        return v[0:8] + v[8:16] + v[16:24]

    full, tail = slice(0, LANES), slice(channels, channels + LANES)
    stats = {0: [stat(st_ref, full), stat(st_peer_ref, full)]}
    for o in (-2, -1, 1, 2):
        k = (-o) % n_tile
        stats[o] = [stat(near[k - 1], tail), stat(far[k - 1], tail)] if k else stats[0]
    chan = merged_stats(stats, tile, n_tile, float(count), group_of_channel(channels))
    gain = gain_ref[...] * (1.0 + temb_ref[:, :channels])
    shift = temb_ref[:, channels:]
    n = normed_ref.shape[0] // 2
    fill_normed(canvas_ref, slice(0, n), (chan, gain, shift), normed_ref, (0, -1))
    chan_ref[...] = chan
    q_ref[...] = (jnp.dot(normed_ref[...], wq_ref[...], preferred_element_type=F32).astype(BF16)) * 0.125

    own_rows = thumb_ref.shape[0]
    all_ref[:own_rows, :] = thumb_ref[...]
    for i, ref in enumerate(near + far):
        all_ref[own_rows + i * half : own_rows + (i + 1) * half, :] = ref[:, :channels]
    k_ref[...] = jnp.dot(all_ref[...], wk_ref[...], preferred_element_type=F32).astype(BF16)
    v_ref[...] = jnp.dot(all_ref[...], wv_ref[...], preferred_element_type=F32).astype(BF16)
    weights = row_weights(ramps_ref, tile, n_tile, columns, True)
    attend(lambda cols: q_ref[:, cols], k_ref, v_ref, wo_ref, weights, bl_ref, send_ref, own_ref, split)


def second_block(n_tile, split, columns, *refs):
    ramps_ref, canvas_ref, temb_ref, gain_ref, wq_ref, wo_ref, k_ref, v_ref, chan_ref = refs[:9]
    if split:
        send_ref, own_ref, normed_ref, q_ref, bl_ref = refs[9:]
    else:
        send_ref, normed_ref, q_ref, bl_ref = refs[9:]
        own_ref = None
    channels = canvas_ref.shape[1]
    tile = lax.axis_index("tile")
    gain = gain_ref[...] * (1.0 + temb_ref[:, :channels])
    shift = temb_ref[:, channels:]
    n = normed_ref.shape[0] // 2
    fill_normed(canvas_ref, slice(n, 2 * n), (chan_ref[...], gain, shift), normed_ref, (0, 1))
    q_ref[...] = (jnp.dot(normed_ref[...], wq_ref[...], preferred_element_type=F32).astype(BF16)) * 0.125
    weights = row_weights(ramps_ref, tile, n_tile, columns, False)
    attend(lambda cols: q_ref[:, cols], k_ref, v_ref, wo_ref, weights, bl_ref, send_ref, own_ref, split)


def add_up(own_a, got_a, own_b, got_b, out_ref):
    n = own_a.shape[0]
    out_ref[:n, :] = (own_a[...].astype(F32) + got_a[...].astype(F32)).astype(BF16)
    out_ref[n:, :] = (own_b[...].astype(F32) + got_b[...].astype(F32)).astype(BF16)


def shifted(value, axis, step):
    count = lax.axis_size(axis)
    return lax.ppermute(value, axis, [(i, (i + step) % count) for i in range(count)])


def on_device(canvas, thumb, ramps, t_embed, norm_gain, w_query, w_key, w_value, w_out):
    owned, columns, channels = canvas.shape
    n_tile, n_chan, n_sub = (lax.axis_size(a) for a in ("tile", "chan", "sub"))
    assert owned == 2 * M and n_sub == 2
    local_ch = w_query.shape[1]
    width = -(-local_ch // LANES) * LANES
    if width != local_ch:
        grow = width - local_ch
        w_query, w_key, w_value = (jnp.pad(w, ((0, 0), (0, grow))) for w in (w_query, w_key, w_value))
        w_out = jnp.pad(w_out, ((0, grow), (0, 0)))
    rows = owned * columns
    n = rows // 2
    x = canvas.reshape(rows, channels)
    half = thumb.shape[0] // n_sub
    tokens = thumb.shape[0] * n_tile
    count = n * (channels // GROUPS)
    split = n_chan == 2 and (channels // 2) % LANES == 0
    vmem = pl.BlockSpec(memory_space=pltpu.VMEM)
    smem = pl.BlockSpec(memory_space=pltpu.SMEM)

    payload, st = pl.pallas_call(
        local_stats,
        out_shape=(
            jax.ShapeDtypeStruct((half, channels + LANES), BF16),
            jax.ShapeDtypeStruct((half, LANES), BF16),
        ),
        in_specs=[vmem, vmem],
        out_specs=(vmem, vmem),
        name="local_stats",
    )(x, thumb)

    if n_tile <= 4:
        near = [shifted(payload, "tile", k) for k in range(1, n_tile)]
    else:
        every = lax.all_gather(payload, "tile", axis=0)
        me = lax.axis_index("tile")
        near = [lax.dynamic_index_in_dim(every, (me - k) % n_tile, 0, False) for k in range(1, n_tile)]
    st_peer = shifted(st, "sub", 1)
    far = [shifted(v, "sub", 1) for v in near]

    temb = t_embed.reshape(1, -1)
    gain = norm_gain.reshape(1, -1)
    part = jax.ShapeDtypeStruct((n, channels // 2 if split else channels), BF16)
    parts = (part, part) if split else (part,)
    work = [
        pltpu.VMEM((2 * n, channels), BF16),
        pltpu.VMEM((2 * n, width), BF16),
        pltpu.VMEM((n, width), BF16),
    ]
    kv = jax.ShapeDtypeStruct((tokens, width), BF16)
    outs = pl.pallas_call(
        functools.partial(first_block, n_tile, split, count, columns),
        out_shape=parts + (kv, kv, jax.ShapeDtypeStruct((8, channels), F32)),
        in_specs=[smem] + [vmem] * (10 + 2 * (n_tile - 1)),
        out_specs=(vmem,) * (len(parts) + 3),
        scratch_shapes=[pltpu.VMEM((tokens, channels), BF16)] + work,
        name="first_block",
    )(ramps, x, thumb, temb, gain, w_query, w_key, w_value, w_out, st, st_peer, *near, *far)
    first, (keys, values, chan) = outs[: len(parts)], outs[len(parts) :]
    got_a = shifted(first[0], "chan", 1) if split else None
    second = pl.pallas_call(
        functools.partial(second_block, n_tile, split, columns),
        out_shape=parts,
        in_specs=[smem] + [vmem] * 8,
        out_specs=(vmem,) * len(parts),
        scratch_shapes=work,
        name="second_block",
    )(ramps, x, temb, gain, w_query, w_out, keys, values, chan)
    if split:
        got_b = shifted(second[0], "chan", 1)
        out = pl.pallas_call(
            add_up,
            out_shape=jax.ShapeDtypeStruct((rows, channels // 2), BF16),
            in_specs=[vmem] * 4,
            out_specs=vmem,
            name="add_up",
        )(first[1], got_a, second[1], got_b)
    else:
        both = jnp.concatenate([first[0], second[0]], axis=0)
        out = lax.psum_scatter(both, "chan", scatter_dimension=1, tiled=True)
    return out.reshape(owned, columns, out.shape[1])


def solution(mesh):
    placed = (
        P(("groups", "tile"), "sub", None),
        P(("groups", "tile"), None),
        P(),
        P("groups"),
        P(),
        P(None, "chan"),
        P(None, "chan"),
        P(None, "chan"),
        P("chan", None),
    )
    return jax.shard_map(
        on_device,
        mesh=mesh,
        in_specs=placed,
        out_specs=P(("groups", "tile"), "sub", "chan"),
        check_vma=False,
    )
```

time: 119 us -> 43.8 us (0.37)
  blocking collectives: 28.6 us -> 0 us
  Pallas kernels: 0 us -> 16.9 us
  waiting for transfers between devices: 28.3 us -> 13.3 us
  local copies, waits for them, and re-layouts: 18.8 us -> 4.51 us
  between operations: 13.7 us -> 0.09 us
  other arithmetic: 10.4 us -> 0 us
  matrix products: 7.22 us -> 0 us
  starting transfers between devices: 11.6 us -> 8.73 us
    all_gather x1 -> x0, blocking collectives: 23.5 us -> none  [on_device(): piece = lax.all_gather(thumb, 'tile', axis=0, tiled=True)]
    unnamed x2 -> x0, waiting for transfers between devices: 22.3 us -> none
    pallas_call x0 -> x4, Pallas kernels: none -> 16.9 us  [the longest x1 7.32 us: on_device(): pl.pallas_call(functools.partial(first_block, n_tile, split, count, colum...]
    concatenate x3 -> x0, local copies, waits for them, and re-layouts: 11.3 us -> none  [extended_2(): x = jnp.concatenate([before, x, after], axis=dim)]
    ppermute x4 -> x9, waiting for transfers between devices: 6 us -> 13.3 us  [shifted(): lax.ppermute(value, axis, [(i, (i + step) % count) for i in range(count)])]
    dot_general x6 -> x0, matrix products: 7.22 us -> none  [the longest x1 2.18 us: on_device(): jnp.dot(piece, w_key, preferred_element_type=jnp.float32)]
    reduce_sum x3 -> x0, other arithmetic: 6.95 us -> none  [the longest x1 3.4 us: on_device(): squares = lax.psum(jnp.sum(centered * centered, axis=(0, 1, 3)), 'sub')]
    psum x2 -> x0, blocking collectives: 5.12 us -> none  [the longest x1 2.65 us: on_device(): squares = lax.psum(jnp.sum(centered * centered, axis=(0, 1, 3)), 'sub')]
  transfers between devices with their start and end apart: 5 -> 9, of which waited for: 3 -> 3; matrix products, arithmetic and copies ran while one was open for 11% -> 6% of each run, Pallas kernels for 0% -> 12%
where the time goes in v1:
time: 43.8 us; the launch traced here: 43.5 us
  Pallas kernels  16.9 us (39%)
  waiting for transfers between devices  13.3 us (30%)
  starting transfers between devices  8.73 us (20%)
  local copies, waits for them, and re-layouts  4.51 us (10%)
    ppermute x9, waiting for transfers between devices, shifted(): lax.ppermute(value, axis, [(i, (i + step) % count) for i in range(count)])  13.3 us
    ppermute x9, starting transfers between devices, shifted(): lax.ppermute(value, axis, [(i, (i + step) % count) for i in range(count)])  8.73 us
    pallas_call x1, Pallas kernels, on_device(): pl.pallas_call(functools.partial(first_block, n_tile, split, count, colum...  7.32 us
    pallas_call x1, Pallas kernels, on_device(): pl.pallas_call(functools.partial(second_block, n_tile, split, columns), o...  5 us
    pallas_call x1, Pallas kernels, on_device(): pl.pallas_call(local_stats, out_shape=(jax.ShapeDtypeStruct((half, channe...  2.6 us
    pallas_call x1, Pallas kernels, on_device(): pl.pallas_call(add_up, out_shape=jax.ShapeDtypeStruct((rows, channels //...  1.95 us
    unnamed x18, local copies, waits for them, and re-layouts  1.91 us
    reshape x1, local copies, waits for them, and re-layouts, on_device(): temb = t_embed.reshape(1, -1)  1.31 us
  transfers between devices with their start and end apart: 9, of which 3 were waited for; matrix products, arithmetic and copies ran while one was open for 6% of the time, Pallas kernels for 12%

profile of v1, /device:TPU:0, one launch (start us, length us, event | category | flops | bytes accessed | tf_op | source)
XLA Modules:
  0.0 43.5 jit_solution(5535417659110811422)
XLA Ops:
  0.0 2.6 %local_stats.1 = (bf16[32,1408]{1,0:T(8,128)(2,1)}, bf16[32,128]{1,0:T(8,128)(2,1)}) custom-call(bf16[256,1280]{1,0:T(8,128)(2,1)} %bitcast.2, bf16[64,1280]{1,0:T(8,128)(2,1)} %refs_2_.1), custom_call_target="tpu_custom_call" | custom-call | tf_op jit(solution)/shard_map/local_stats/pallas_call | solution.py:254
  2.6 5.1 %collective-permute-start.3 = (bf16[32,1408]{1,0:T(8,128)(2,1)}, bf16[32,1408]{1,0:T(8,128)(2,1)S(1)}, u32[]{:S(2)}, u32[]{:S(2)}) collective-permute-start(bf16[32,1408]{1,0:T(8,128)(2,1)} %get-tuple-element.15), channel_id=1, source_target_pairs={{0,12},{4,0},{8,4},{12,8},{1,13},{5,1},{9,5},{13,9},{2,14},{6,2},{... | collective-permute-start | bytes 270344 | tf_op jit(solution)/shard_map/ppermute | solution.py:231
  7.7 0.0 collective-permute-start.2
  7.7 1.0 %collective-permute-start.1 = (bf16[32,1408]{1,0:T(8,128)(2,1)}, bf16[32,1408]{1,0:T(8,128)(2,1)S(1)}, u32[]{:S(2)}, u32[]{:S(2)}) collective-permute-start(bf16[32,1408]{1,0:T(8,128)(2,1)} %get-tuple-element.15), channel_id=1, source_target_pairs={{0,4},{4,8},{8,12},{12,0},{1,5},{5,9},{9,13},{13,1},{2,6},{6,10},{... | collective-permute-start | bytes 270344 | tf_op jit(solution)/shard_map/ppermute | solution.py:231
  8.7 2.3 %collective-permute-done.3.refs_13_ = bf16[32,1408]{1,0:T(8,128)(2,1)S(1)} collective-permute-done((bf16[32,1408]{1,0:T(8,128)(2,1)}, bf16[32,1408]{1,0:T(8,128)(2,1)S(1)}, u32[]{:S(2)}, u32[]{:S(2)}) %collective-permute-start.3) | collective-permute-done | bytes 90144 | tf_op jit(solution)/shard_map/ppermute | solution.py:231
  11.0 0.0 copy-start.2
  11.0 0.0 collective-permute-start.6
  11.0 5.0 %collective-permute-done.2.refs_12_ = bf16[32,1408]{1,0:T(8,128)(2,1)S(1)} collective-permute-done((bf16[32,1408]{1,0:T(8,128)(2,1)}, bf16[32,1408]{1,0:T(8,128)(2,1)S(1)}, u32[]{:S(2)}, u32[]{:S(2)}) %collective-permute-start.2) | collective-permute-done | bytes 90144 | tf_op jit(solution)/shard_map/ppermute | solution.py:231
  16.0 0.0 copy-start.3
  16.0 0.0 collective-permute-start.5
  16.0 0.0 collective-permute-done.1.refs_11_
  16.0 0.0 copy-start.4
  16.1 0.5 %collective-permute-start.4 = (bf16[32,1408]{1,0:T(8,128)(2,1)S(1)}, bf16[32,1408]{1,0:T(8,128)(2,1)S(1)}, u32[]{:S(2)}, u32[]{:S(2)}) collective-permute-start(bf16[32,1408]{1,0:T(8,128)(2,1)S(1)} %collective-permute-done.1.refs_11_), channel_id=1, source_target_pairs={{0,1},{1,0},{2,3},{3,2},{4,5},{5,4},{6,7},{7,6},{8,9},{9,8},{10,11... | collective-permute-start | bytes 270344 | tf_op jit(solution)/shard_map/ppermute | solution.py:231
  16.6 0.1 collective-permute-start
  16.6 1.3 %reshape.14.refs_4_.refs_3_ = f32[1,1280]{1,0:T(1,128)} reshape(f32[1280]{0:T(1024)} %param.13) | data formatting | bytes 10240 | tf_op jit(solution)/shard_map/reshape | solution.py:275
  17.9 1.3 %reshape.13.refs_3_.refs_2_ = f32[1,2560]{1,0:T(1,128)} reshape(f32[2560]{0:T(1024)} %param.12) | data formatting | bytes 20480 | tf_op jit(solution)/shard_map/reshape | solution.py:274
  19.2 0.0 collective-permute-done.refs_10_
  19.2 0.0 copy-start.8
  19.2 0.0 collective-permute-done.6.refs_16_
  19.2 0.0 copy-start.5
  19.3 0.0 collective-permute-done.5.refs_15_
  19.3 0.0 copy-start.6
  19.3 0.0 collective-permute-done.4.refs_14_
  19.3 0.0 copy-done.2
  19.3 0.0 copy-done.3
  19.3 0.0 copy-done.4
  19.3 0.5 %copy-done.8 = bf16[32,128]{1,0:T(8,128)(2,1)} copy-done((bf16[32,128]{1,0:T(8,128)(2,1)}, bf16[32,128]{1,0:T(8,128)(2,1)S(1)}, u32[]{:S(2)}) %copy-start.8) | copy-done | bytes 8216
  19.8 0.0 copy-done.5
  19.9 0.0 copy-done.6
  19.9 0.0 copy-start.7
  19.9 0.6 %copy-done.7 = bf16[32,1408]{1,0:T(8,128)(2,1)} copy-done((bf16[32,1408]{1,0:T(8,128)(2,1)}, bf16[32,1408]{1,0:T(8,128)(2,1)S(1)}, u32[]{:S(2)}) %copy-start.7) | copy-done | bytes 90136
  20.5 7.3 %first_block.1 = (bf16[128,640]{1,0:T(8,128)(2,1)}, bf16[128,640]{1,0:T(8,128)(2,1)}, bf16[256,640]{1,0:T(8,128)(2,1)}, bf16[256,640]{1,0:T(8,128)(2,1)}, f32[8,1280]{1,0:T(8,128)}) custom-call(s32[4,16]{1,0:T(4,128)} %refs_0_.3, bf16[256,1280]{1,0:T(8,128)(2,1)} %bitcast.3, bf16[64,1280]{1,0:T(8,128)(2,1)} %refs_2_.1, f32[1,2560]{1,0:T(1,128)} %reshape.13.refs_3_.refs_2_, ...), custom_call_target="tpu_custom_call" | custom-call | tf_op jit(solution)/shard_map/first_block/pallas_call | solution.py:284
  27.9 1.5 %collective-permute-start.7 = (bf16[128,640]{1,0:T(8,128)(2,1)}, bf16[128,640]{1,0:T(8,128)(2,1)S(1)}, u32[]{:S(2)}, u32[]{:S(2)}) collective-permute-start(bf16[128,640]{1,0:T(8,128)(2,1)} %get-tuple-element.17), channel_id=1, source_target_pairs={{0,2},{2,0},{1,3},{3,1},{4,6},{6,4},{5,7},{7,5},{8,10},{10,8},{9,1... | collective-permute-start | bytes 491528 | tf_op jit(solution)/shard_map/ppermute | solution.py:231
  29.4 5.0 %second_block.1 = (bf16[128,640]{1,0:T(8,128)(2,1)}, bf16[128,640]{1,0:T(8,128)(2,1)}) custom-call(s32[4,16]{1,0:T(4,128)} %refs_0_.3, bf16[256,1280]{1,0:T(8,128)(2,1)} %bitcast.4, f32[1,2560]{1,0:T(1,128)} %reshape.13.refs_3_.refs_2_, f32[1,1280]{1,0:T(1,128)} %reshape.14.refs_4_.refs_3_, bf16[1280,640]{1,0:T(8,128)(2,1)} %refs_4_.1, ...), custom_call_target="tpu_custom_call" | custom-call | tf_op jit(solution)/shard_map/second_block/pallas_call | solution.py:294
  34.4 0.5 %collective-permute-start.8 = (bf16[128,640]{1,0:T(8,128)(2,1)}, bf16[128,640]{1,0:T(8,128)(2,1)S(1)}, u32[]{:S(2)}, u32[]{:S(2)}) collective-permute-start(bf16[128,640]{1,0:T(8,128)(2,1)} %get-tuple-element.22), channel_id=1, source_target_pairs={{0,2},{2,0},{1,3},{3,1},{4,6},{6,4},{5,7},{7,5},{8,10},{10,8},{9,1... | collective-permute-start | bytes 491528 | tf_op jit(solution)/shard_map/ppermute | solution.py:231
  34.9 0.0 collective-permute-done.7.got_a
  34.9 0.0 copy-start
  34.9 5.9 %collective-permute-done.8.got_b = bf16[128,640]{1,0:T(8,128)(2,1)S(1)} collective-permute-done((bf16[128,640]{1,0:T(8,128)(2,1)}, bf16[128,640]{1,0:T(8,128)(2,1)S(1)}, u32[]{:S(2)}, u32[]{:S(2)}) %collective-permute-start.8) | collective-permute-done | bytes 163872 | tf_op jit(solution)/shard_map/ppermute | solution.py:231
  40.9 0.0 copy-start.1
  40.9 0.0 copy-done
  40.9 0.7 %copy-done.1 = bf16[128,640]{1,0:T(8,128)(2,1)} copy-done((bf16[128,640]{1,0:T(8,128)(2,1)}, bf16[128,640]{1,0:T(8,128)(2,1)S(1)}, u32[]{:S(2)}) %copy-start.1) | copy-done | bytes 163864
  41.5 2.0 %add_up.1 = bf16[256,640]{1,0:T(8,128)(2,1)} custom-call(bf16[128,640]{1,0:T(8,128)(2,1)} %get-tuple-element.16.own_a, bf16[128,640]{1,0:T(8,128)(2,1)} %copy-done, bf16[128,640]{1,0:T(8,128)(2,1)} %get-tuple-element.21.own_b, bf16[128,640]{1,0:T(8,128)(2,1)} %copy-done.1), custom_call_target="tpu_custom_call" | custom-call | tf_op jit(solution)/shard_map/add_up/pallas_call | solution.py:304
Async XLA Ops:
  2.6 8.4 %collective-permute-start.3 = (bf16[32,1408]{1,0:T(8,128)(2,1)}, bf16[32,1408]{1,0:T(8,128)(2,1)S(1)}, u32[]{:S(2)}, u32[]{:S(2)}) collective-permute-start(bf16[32,1408]{1,0:T(8,128)(2,1)} %get-tuple-element.15), channel_id=1, source_target_pairs={{0,12},{4,0},{8,4},{12,8},{1,13},{5,1},{9,5},{13,9},{2,14},{6,2},{... | collective-permute-start | bytes 270344 | tf_op jit(solution)/shard_map/ppermute | solution.py:231
  7.7 8.4 %collective-permute-start.2 = (bf16[32,1408]{1,0:T(8,128)(2,1)}, bf16[32,1408]{1,0:T(8,128)(2,1)S(1)}, u32[]{:S(2)}, u32[]{:S(2)}) collective-permute-start(bf16[32,1408]{1,0:T(8,128)(2,1)} %get-tuple-element.15), channel_id=1, source_target_pairs={{0,8},{4,12},{8,0},{12,4},{1,9},{5,13},{9,1},{13,5},{2,10},{6,14},... | collective-permute-start | bytes 270344 | tf_op jit(solution)/shard_map/ppermute | solution.py:231
  7.7 8.4 %collective-permute-start.1 = (bf16[32,1408]{1,0:T(8,128)(2,1)}, bf16[32,1408]{1,0:T(8,128)(2,1)S(1)}, u32[]{:S(2)}, u32[]{:S(2)}) collective-permute-start(bf16[32,1408]{1,0:T(8,128)(2,1)} %get-tuple-element.15), channel_id=1, source_target_pairs={{0,4},{4,8},{8,12},{12,0},{1,5},{5,9},{9,13},{13,1},{2,6},{6,10},{... | collective-permute-start | bytes 270344 | tf_op jit(solution)/shard_map/ppermute | solution.py:231
  11.0 8.3 %copy-start.2 = (bf16[32,1408]{1,0:T(8,128)(2,1)}, bf16[32,1408]{1,0:T(8,128)(2,1)S(1)}, u32[]{:S(2)}) copy-start(bf16[32,1408]{1,0:T(8,128)(2,1)S(1)} %collective-permute-done.3.refs_13_) | copy-start | bytes 270340
  11.0 8.2 %collective-permute-start.6 = (bf16[32,1408]{1,0:T(8,128)(2,1)S(1)}, bf16[32,1408]{1,0:T(8,128)(2,1)S(1)}, u32[]{:S(2)}, u32[]{:S(2)}) collective-permute-start(bf16[32,1408]{1,0:T(8,128)(2,1)S(1)} %collective-permute-done.3.refs_13_), channel_id=1, source_target_pairs={{0,1},{1,0},{2,3},{3,2},{4,5},{5,4},{6,7},{7,6},{8,9},{9,8},{10,11... | collective-permute-start | bytes 270344 | tf_op jit(solution)/shard_map/ppermute | solution.py:231
  16.0 3.3 %copy-start.3 = (bf16[32,1408]{1,0:T(8,128)(2,1)}, bf16[32,1408]{1,0:T(8,128)(2,1)S(1)}, u32[]{:S(2)}) copy-start(bf16[32,1408]{1,0:T(8,128)(2,1)S(1)} %collective-permute-done.2.refs_12_) | copy-start | bytes 270340
  16.0 3.2 %collective-permute-start.5 = (bf16[32,1408]{1,0:T(8,128)(2,1)S(1)}, bf16[32,1408]{1,0:T(8,128)(2,1)S(1)}, u32[]{:S(2)}, u32[]{:S(2)}) collective-permute-start(bf16[32,1408]{1,0:T(8,128)(2,1)S(1)} %collective-permute-done.2.refs_12_), channel_id=1, source_target_pairs={{0,1},{1,0},{2,3},{3,2},{4,5},{5,4},{6,7},{7,6},{8,9},{9,8},{10,11... | collective-permute-start | bytes 270344 | tf_op jit(solution)/shard_map/ppermute | solution.py:231
  16.0 3.3 %copy-start.4 = (bf16[32,1408]{1,0:T(8,128)(2,1)}, bf16[32,1408]{1,0:T(8,128)(2,1)S(1)}, u32[]{:S(2)}) copy-start(bf16[32,1408]{1,0:T(8,128)(2,1)S(1)} %collective-permute-done.1.refs_11_) | copy-start | bytes 270340
  16.1 3.2 %collective-permute-start.4 = (bf16[32,1408]{1,0:T(8,128)(2,1)S(1)}, bf16[32,1408]{1,0:T(8,128)(2,1)S(1)}, u32[]{:S(2)}, u32[]{:S(2)}) collective-permute-start(bf16[32,1408]{1,0:T(8,128)(2,1)S(1)} %collective-permute-done.1.refs_11_), channel_id=1, source_target_pairs={{0,1},{1,0},{2,3},{3,2},{4,5},{5,4},{6,7},{7,6},{8,9},{9,8},{10,11... | collective-permute-start | bytes 270344 | tf_op jit(solution)/shard_map/ppermute | solution.py:231
  16.6 2.7 %collective-permute-start = (bf16[32,128]{1,0:T(8,128)(2,1)}, bf16[32,128]{1,0:T(8,128)(2,1)S(1)}, u32[]{:S(2)}, u32[]{:S(2)}) collective-permute-start(bf16[32,128]{1,0:T(8,128)(2,1)} %get-tuple-element.14.refs_9_), channel_id=1, source_target_pairs={{0,1},{1,0},{2,3},{3,2},{4,5},{5,4},{6,7},{7,6},{8,9},{9,8},{10,11... | collective-permute-start | bytes 24584 | tf_op jit(solution)/shard_map/ppermute | solution.py:231
  19.2 0.6 %copy-start.8 = (bf16[32,128]{1,0:T(8,128)(2,1)}, bf16[32,128]{1,0:T(8,128)(2,1)S(1)}, u32[]{:S(2)}) copy-start(bf16[32,128]{1,0:T(8,128)(2,1)S(1)} %collective-permute-done.refs_10_) | copy-start | bytes 24580
  19.2 0.6 %copy-start.5 = (bf16[32,1408]{1,0:T(8,128)(2,1)}, bf16[32,1408]{1,0:T(8,128)(2,1)S(1)}, u32[]{:S(2)}) copy-start(bf16[32,1408]{1,0:T(8,128)(2,1)S(1)} %collective-permute-done.6.refs_16_) | copy-start | bytes 270340
  19.3 0.7 %copy-start.6 = (bf16[32,1408]{1,0:T(8,128)(2,1)}, bf16[32,1408]{1,0:T(8,128)(2,1)S(1)}, u32[]{:S(2)}) copy-start(bf16[32,1408]{1,0:T(8,128)(2,1)S(1)} %collective-permute-done.5.refs_15_) | copy-start | bytes 270340
  19.9 0.6 %copy-start.7 = (bf16[32,1408]{1,0:T(8,128)(2,1)}, bf16[32,1408]{1,0:T(8,128)(2,1)S(1)}, u32[]{:S(2)}) copy-start(bf16[32,1408]{1,0:T(8,128)(2,1)S(1)} %collective-permute-done.4.refs_14_) | copy-start | bytes 270340
  27.9 7.1 %collective-permute-start.7 = (bf16[128,640]{1,0:T(8,128)(2,1)}, bf16[128,640]{1,0:T(8,128)(2,1)S(1)}, u32[]{:S(2)}, u32[]{:S(2)}) collective-permute-start(bf16[128,640]{1,0:T(8,128)(2,1)} %get-tuple-element.17), channel_id=1, source_target_pairs={{0,2},{2,0},{1,3},{3,1},{4,6},{6,4},{5,7},{7,5},{8,10},{10,8},{9,1... | collective-permute-start | bytes 491528 | tf_op jit(solution)/shard_map/ppermute | solution.py:231
  34.4 6.5 %collective-permute-start.8 = (bf16[128,640]{1,0:T(8,128)(2,1)}, bf16[128,640]{1,0:T(8,128)(2,1)S(1)}, u32[]{:S(2)}, u32[]{:S(2)}) collective-permute-start(bf16[128,640]{1,0:T(8,128)(2,1)} %get-tuple-element.22), channel_id=1, source_target_pairs={{0,2},{2,0},{1,3},{3,1},{4,6},{6,4},{5,7},{7,5},{8,10},{10,8},{9,1... | collective-permute-start | bytes 491528 | tf_op jit(solution)/shard_map/ppermute | solution.py:231
  34.9 5.9 %copy-start = (bf16[128,640]{1,0:T(8,128)(2,1)}, bf16[128,640]{1,0:T(8,128)(2,1)S(1)}, u32[]{:S(2)}) copy-start(bf16[128,640]{1,0:T(8,128)(2,1)S(1)} %collective-permute-done.7.got_a) | copy-start | bytes 491524
  40.9 0.7 %copy-start.1 = (bf16[128,640]{1,0:T(8,128)(2,1)}, bf16[128,640]{1,0:T(8,128)(2,1)S(1)}, u32[]{:S(2)}) copy-start(bf16[128,640]{1,0:T(8,128)(2,1)S(1)} %collective-permute-done.8.got_b) | copy-start | bytes 491524

commit v2 on v1

--- a/solution.py
+++ b/solution.py
@@ -6,6 +6,7 @@
 from jax.experimental import pallas as pl
 from jax.experimental.pallas import tpu as pltpu
 from jax.sharding import PartitionSpec as P
+
 
 HD = 64
 GROUPS = 32
@@ -46,16 +47,21 @@
     return out
 
 
-def local_stats(canvas_ref, thumb_ref, pay_ref, st_ref):
+def local_stats(canvas_hbm, thumb_hbm, pay_ref, st_ref, canvas_ref, thumb_ref, sems):
     channels = canvas_ref.shape[1]
     half = pay_ref.shape[0]
     n = canvas_ref.shape[0] // 2
     size = channels // GROUPS
-    sub = lax.axis_index("sub")
-    start = pl.multiple_of(sub * half, half)
-    pay_ref[:, :channels] = thumb_ref[pl.ds(start, half), :]
+    loads = []
+    for b in range(2):
+        rows = pl.ds(b * n, n)
+        loads.append(pltpu.make_async_copy(canvas_hbm.at[rows], canvas_ref.at[rows], sems.at[b]))
+    loads.append(pltpu.make_async_copy(thumb_hbm, thumb_ref, sems.at[2]))
+    for load in loads:
+        load.start()
     means, squares = [], []
     for b in range(2):
+        loads[b].wait()
         x = canvas_ref[b * n : (b + 1) * n, :].astype(F32)
         mean = jnp.sum(x, axis=0, keepdims=True) * (1.0 / n)
         c = x - mean
@@ -74,6 +80,23 @@
     block = jnp.concatenate(list(parts) + [pad], axis=0).astype(BF16)
     pay_ref[:, channels:] = block
     st_ref[...] = block
+    loads[2].wait()
+    start = pl.multiple_of(lax.axis_index("sub") * half, half)
+    pay_ref[:, :channels] = thumb_ref[pl.ds(start, half), :]
+
+
+def meanwhile(thumb_ref, *refs):
+    count = (len(refs) - 3) // 2
+    hbm, vmem = refs[:count], refs[count : 2 * count]
+    k_ref, v_ref, sems = refs[2 * count :]
+    loads = [pltpu.make_async_copy(a, b, sems.at[i]) for i, (a, b) in enumerate(zip(hbm, vmem))]
+    for load in loads:
+        load.start()
+    for i, out in enumerate((k_ref, v_ref)):
+        loads[i].wait()
+        out[...] = jnp.dot(thumb_ref[...], vmem[i][...], preferred_element_type=F32).astype(BF16)
+    for load in loads[2:]:
+        load.wait()
 
 
 def row_weights(ramps_ref, tile, n_tile, columns, upper):
@@ -152,6 +175,16 @@
     return exact_dot(rows_of(rows, LANES), member, (((1,), (0,)), ((), ())))
 
 
+def in_one_row(ref, first, last):
+    return jnp.concatenate([ref[i : i + 1, :] for i in range(first, last)], axis=1)
+
+
+def gain_and_shift(temb_ref, gain_ref):
+    n = gain_ref.shape[0]
+    gain = in_one_row(gain_ref, 0, n) * (1.0 + in_one_row(temb_ref, 0, n))
+    return gain, in_one_row(temb_ref, n, 2 * n)
+
+
 def fill_normed(canvas_ref, rows, affine, normed_ref, order):
     chan, gain, shift = affine
     n = normed_ref.shape[0] // 2
@@ -162,10 +195,11 @@
 
 
 def first_block(n_tile, split, count, columns, *refs):
-    (ramps_ref, canvas_ref, thumb_ref, temb_ref, gain_ref, wq_ref, wk_ref, wv_ref, wo_ref, st_ref, st_peer_ref) = refs[:11]
-    near = refs[11 : 11 + n_tile - 1]
-    far = refs[11 + n_tile - 1 : 11 + 2 * (n_tile - 1)]
-    rest = refs[11 + 2 * (n_tile - 1) :]
+    (ramps_ref, canvas_ref, k_own_ref, v_own_ref, temb_ref, gain_ref, wq_ref, wk_ref, wv_ref, wo_ref) = refs[:10]
+    st_ref, st_peer_ref = refs[10:12]
+    near = refs[12 : 12 + n_tile - 1]
+    far = refs[12 + n_tile - 1 : 12 + 2 * (n_tile - 1)]
+    rest = refs[12 + 2 * (n_tile - 1) :]
     if split:
         send_ref, own_ref, k_ref, v_ref, chan_ref, all_ref, normed_ref, q_ref, bl_ref = rest
     else:
@@ -185,19 +219,18 @@
         k = (-o) % n_tile
         stats[o] = [stat(near[k - 1], tail), stat(far[k - 1], tail)] if k else stats[0]
     chan = merged_stats(stats, tile, n_tile, float(count), group_of_channel(channels))
-    gain = gain_ref[...] * (1.0 + temb_ref[:, :channels])
-    shift = temb_ref[:, channels:]
+    gain, shift = gain_and_shift(temb_ref, gain_ref)
     n = normed_ref.shape[0] // 2
     fill_normed(canvas_ref, slice(0, n), (chan, gain, shift), normed_ref, (0, -1))
     chan_ref[...] = chan
     q_ref[...] = (jnp.dot(normed_ref[...], wq_ref[...], preferred_element_type=F32).astype(BF16)) * 0.125
 
-    own_rows = thumb_ref.shape[0]
-    all_ref[:own_rows, :] = thumb_ref[...]
+    own_rows = k_own_ref.shape[0]
     for i, ref in enumerate(near + far):
-        all_ref[own_rows + i * half : own_rows + (i + 1) * half, :] = ref[:, :channels]
-    k_ref[...] = jnp.dot(all_ref[...], wk_ref[...], preferred_element_type=F32).astype(BF16)
-    v_ref[...] = jnp.dot(all_ref[...], wv_ref[...], preferred_element_type=F32).astype(BF16)
+        all_ref[i * half : (i + 1) * half, :] = ref[:, :channels]
+    k_ref[:own_rows, :], v_ref[:own_rows, :] = k_own_ref[...], v_own_ref[...]
+    k_ref[own_rows:, :] = jnp.dot(all_ref[...], wk_ref[...], preferred_element_type=F32).astype(BF16)
+    v_ref[own_rows:, :] = jnp.dot(all_ref[...], wv_ref[...], preferred_element_type=F32).astype(BF16)
     weights = row_weights(ramps_ref, tile, n_tile, columns, True)
     attend(lambda cols: q_ref[:, cols], k_ref, v_ref, wo_ref, weights, bl_ref, send_ref, own_ref, split)
 
@@ -209,10 +242,8 @@
     else:
         send_ref, normed_ref, q_ref, bl_ref = refs[9:]
         own_ref = None
-    channels = canvas_ref.shape[1]
     tile = lax.axis_index("tile")
-    gain = gain_ref[...] * (1.0 + temb_ref[:, :channels])
-    shift = temb_ref[:, channels:]
+    gain, shift = gain_and_shift(temb_ref, gain_ref)
     n = normed_ref.shape[0] // 2
     fill_normed(canvas_ref, slice(n, 2 * n), (chan_ref[...], gain, shift), normed_ref, (0, 1))
     q_ref[...] = (jnp.dot(normed_ref[...], wq_ref[...], preferred_element_type=F32).astype(BF16)) * 0.125
@@ -224,6 +255,14 @@
     n = own_a.shape[0]
     out_ref[:n, :] = (own_a[...].astype(F32) + got_a[...].astype(F32)).astype(BF16)
     out_ref[n:, :] = (own_b[...].astype(F32) + got_b[...].astype(F32)).astype(BF16)
+
+
+def resident(*arrays):
+    return [pltpu.with_memory_space_constraint(v, pltpu.VMEM) for v in arrays]
+
+
+def in_hbm(*arrays):
+    return [pltpu.with_memory_space_constraint(v, pltpu.HBM) for v in arrays]
 
 
 def shifted(value, axis, step):
@@ -251,16 +290,37 @@
     vmem = pl.BlockSpec(memory_space=pltpu.VMEM)
     smem = pl.BlockSpec(memory_space=pltpu.SMEM)
 
-    payload, st = pl.pallas_call(
+    hbm = pl.BlockSpec(memory_space=pltpu.HBM)
+    payload, st, x, thumb = pl.pallas_call(
         local_stats,
         out_shape=(
-            jax.ShapeDtypeStruct((half, channels + LANES), BF16),
-            jax.ShapeDtypeStruct((half, LANES), BF16),
+            pltpu.VMEM((half, channels + LANES), BF16),
+            pltpu.VMEM((half, LANES), BF16),
+            pltpu.VMEM(x.shape, BF16),
+            pltpu.VMEM(thumb.shape, BF16),
         ),
-        in_specs=[vmem, vmem],
-        out_specs=(vmem, vmem),
+        in_specs=[hbm, hbm],
+        out_specs=(vmem,) * 4,
+        scratch_shapes=[pltpu.SemaphoreType.DMA((3,))],
+        compiler_params=pltpu.CompilerParams(vmem_limit_bytes=8 << 20),
         name="local_stats",
-    )(x, thumb)
+    )(*in_hbm(x, thumb))
+    x, thumb = resident(x, thumb)
+    temb = t_embed.reshape(-1, LANES)
+    gain = norm_gain.reshape(-1, LANES)
+    brought = (w_key, w_value, w_query, w_out, temb, gain)
+    own_kv = pltpu.VMEM((thumb.shape[0], width), BF16)
+    bring = pl.pallas_call(
+        meanwhile,
+        out_shape=tuple(pltpu.VMEM(v.shape, v.dtype) for v in brought) + (own_kv, own_kv),
+        in_specs=[vmem] + [hbm] * len(brought),
+        out_specs=(vmem,) * (len(brought) + 2),
+        scratch_shapes=[pltpu.SemaphoreType.DMA((len(brought),))],
+        compiler_params=pltpu.CompilerParams(vmem_limit_bytes=8 << 20),
+        name="meanwhile",
+    )
+    *brought, k_own, v_own = bring(thumb, *in_hbm(*brought))
+    w_key, w_value, w_query, w_out, temb, gain, k_own, v_own = resident(*brought, k_own, v_own)
 
     if n_tile <= 4:
         near = [shifted(payload, "tile", k) for k in range(1, n_tile)]
@@ -271,24 +331,26 @@
     st_peer = shifted(st, "sub", 1)
     far = [shifted(v, "sub", 1) for v in near]
 
-    temb = t_embed.reshape(1, -1)
-    gain = norm_gain.reshape(1, -1)
-    part = jax.ShapeDtypeStruct((n, channels // 2 if split else channels), BF16)
+    part = pltpu.VMEM((n, channels // 2 if split else channels), BF16)
     parts = (part, part) if split else (part,)
     work = [
         pltpu.VMEM((2 * n, channels), BF16),
         pltpu.VMEM((2 * n, width), BF16),
         pltpu.VMEM((n, width), BF16),
     ]
-    kv = jax.ShapeDtypeStruct((tokens, width), BF16)
+    kv = pltpu.VMEM((tokens, width), BF16)
     outs = pl.pallas_call(
         functools.partial(first_block, n_tile, split, count, columns),
-        out_shape=parts + (kv, kv, jax.ShapeDtypeStruct((8, channels), F32)),
-        in_specs=[smem] + [vmem] * (10 + 2 * (n_tile - 1)),
+        out_shape=parts + (kv, kv, pltpu.VMEM((8, channels), F32)),
+        in_specs=[smem] + [vmem] * (11 + 2 * (n_tile - 1)),
         out_specs=(vmem,) * (len(parts) + 3),
-        scratch_shapes=[pltpu.VMEM((tokens, channels), BF16)] + work,
+        scratch_shapes=[pltpu.VMEM((tokens - thumb.shape[0], channels), BF16)] + work,
+        compiler_params=pltpu.CompilerParams(vmem_limit_bytes=24 << 20),
         name="first_block",
-    )(ramps, x, thumb, temb, gain, w_query, w_key, w_value, w_out, st, st_peer, *near, *far)
+    )(
+        *(ramps, x, k_own, v_own, temb, gain, w_query, w_key, w_value, w_out),
+        *resident(st, st_peer, *near, *far),
+    )
     first, (keys, values, chan) = outs[: len(parts)], outs[len(parts) :]
     got_a = shifted(first[0], "chan", 1) if split else None
     second = pl.pallas_call(
@@ -297,8 +359,9 @@
         in_specs=[smem] + [vmem] * 8,
         out_specs=(vmem,) * len(parts),
         scratch_shapes=work,
+        compiler_params=pltpu.CompilerParams(vmem_limit_bytes=20 << 20),
         name="second_block",
-    )(ramps, x, temb, gain, w_query, w_out, keys, values, chan)
+    )(ramps, x, temb, gain, w_query, w_out, *resident(keys, values, chan))
     if split:
         got_b = shifted(second[0], "chan", 1)
         out = pl.pallas_call(
@@ -306,8 +369,9 @@
             out_shape=jax.ShapeDtypeStruct((rows, channels // 2), BF16),
             in_specs=[vmem] * 4,
             out_specs=vmem,
-            name="add_up",
-        )(first[1], got_a, second[1], got_b)
+            compiler_params=pltpu.CompilerParams(vmem_limit_bytes=4 << 20),
+        name="add_up",
+        )(*resident(first[1], got_a, second[1], got_b))
     else:
         both = jnp.concatenate([first[0], second[0]], axis=0)
         out = lax.psum_scatter(both, "chan", scatter_dimension=1, tiled=True)

time: 43.8 us -> 34 us (0.78)
  Pallas kernels: 16.9 us -> 12.1 us
  local copies, waits for them, and re-layouts: 4.51 us -> 0.01 us
    pallas_call x1, Pallas kernels: 7.32 us -> 3.71 us  [on_device(): pl.pallas_call(functools.partial(first_block, n_tile, split, count, colum...]
    reshape x2 -> x0, local copies, waits for them, and re-layouts: 2.6 us -> none  [the longest x1 1.31 us: on_device(): temb = t_embed.reshape(1, -1)]
    pallas_call x1, Pallas kernels: 5 us -> 2.62 us  [on_device(): pl.pallas_call(functools.partial(second_block, n_tile, split, columns), o...]
    pallas_call x1 -> x2, Pallas kernels: 2.6 us -> 4.93 us  [the longest x1 2.98 us: on_device(): *brought, k_own, v_own = bring(thumb, *in_hbm(*brought))]
    unnamed x18 -> x2, local copies, waits for them, and re-layouts: 1.91 us -> 0.01 us
    pallas_call x1, Pallas kernels: 1.95 us -> 0.81 us  [on_device(): pl.pallas_call(add_up, out_shape=jax.ShapeDtypeStruct((rows, channels //...]
  transfers between devices with their start and end apart: 9 -> 9, of which waited for: 3 -> 4; matrix products, arithmetic and copies ran while one was open for 6% -> 0% of each run, Pallas kernels for 12% -> 17%
where the time goes in v2:
time: 34 us; the launch traced here: 33.9 us
  waiting for transfers between devices  12.9 us (38%)
  Pallas kernels  12.1 us (36%)
  starting transfers between devices  8.8 us (26%)
    ppermute x9, waiting for transfers between devices, shifted(): lax.ppermute(value, axis, [(i, (i + step) % count) for i in range(count)])  12.9 us
    ppermute x9, starting transfers between devices, shifted(): lax.ppermute(value, axis, [(i, (i + step) % count) for i in range(count)])  8.8 us
    pallas_call x1, Pallas kernels, on_device(): pl.pallas_call(functools.partial(first_block, n_tile, split, count, colum...  3.71 us
    pallas_call x1, Pallas kernels, on_device(): *brought, k_own, v_own = bring(thumb, *in_hbm(*brought))  2.98 us
    pallas_call x1, Pallas kernels, on_device(): pl.pallas_call(functools.partial(second_block, n_tile, split, columns), o...  2.62 us
    pallas_call x1, Pallas kernels, on_device(): pl.pallas_call(local_stats, out_shape=(pltpu.VMEM((half, channels + LANES...  1.95 us
    pallas_call x1, Pallas kernels, on_device(): pl.pallas_call(add_up, out_shape=jax.ShapeDtypeStruct((rows, channels //...  0.81 us
  transfers between devices with their start and end apart: 9, of which 4 were waited for; matrix products, arithmetic and copies ran while one was open for 0% of the time, Pallas kernels for 17%

profile of v2, /device:TPU:0, one launch (start us, length us, event | category | flops | bytes accessed | tf_op | source)
XLA Modules:
  0.0 33.9 jit_solution(13589409628368649280)
XLA Ops:
  0.0 1.9 %local_stats.1 = (bf16[32,1408]{1,0:T(8,128)(2,1)S(1)}, bf16[32,128]{1,0:T(8,128)(2,1)S(1)}, bf16[256,1280]{1,0:T(8,128)(2,1)S(1)}, bf16[64,1280]{1,0:T(8,128)(2,1)S(1)}) custom-call(bf16[256,1280]{1,0:T(8,128)(2,1)} %bitcast.4, bf16[64,1280]{1,0:T(8,128)(2,1)} %thumb_hbm.1), custom_call_target="tpu_custom_call" | custom-call | tf_op jit(solution)/shard_map/local_stats/pallas_call | solution.py:294
  2.0 5.1 %collective-permute-start.3 = (bf16[32,1408]{1,0:T(8,128)(2,1)S(1)}, bf16[32,1408]{1,0:T(8,128)(2,1)S(1)}, u32[]{:S(2)}, u32[]{:S(2)}) collective-permute-start(bf16[32,1408]{1,0:T(8,128)(2,1)S(1)} %get-tuple-element.35), channel_id=1, source_target_pairs={{0,12},{4,0},{8,4},{12,8},{1,13},{5,1},{9,5},{13,9},{2,14},{6,2},{... | collective-permute-start | bytes 270344 | tf_op jit(solution)/shard_map/ppermute | solution.py:270
  7.1 0.0 collective-permute-start.2
  7.1 1.0 %collective-permute-start.1 = (bf16[32,1408]{1,0:T(8,128)(2,1)S(1)}, bf16[32,1408]{1,0:T(8,128)(2,1)S(1)}, u32[]{:S(2)}, u32[]{:S(2)}) collective-permute-start(bf16[32,1408]{1,0:T(8,128)(2,1)S(1)} %get-tuple-element.35), channel_id=1, source_target_pairs={{0,4},{4,8},{8,12},{12,0},{1,5},{5,9},{9,13},{13,1},{2,6},{6,10},{... | collective-permute-start | bytes 270344 | tf_op jit(solution)/shard_map/ppermute | solution.py:270
  8.1 2.0 %collective-permute-done.3.refs_14_ = bf16[32,1408]{1,0:T(8,128)(2,1)S(1)} collective-permute-done((bf16[32,1408]{1,0:T(8,128)(2,1)S(1)}, bf16[32,1408]{1,0:T(8,128)(2,1)S(1)}, u32[]{:S(2)}, u32[]{:S(2)}) %collective-permute-start.3) | collective-permute-done | bytes 90144 | tf_op jit(solution)/shard_map/ppermute | solution.py:270
  10.1 0.0 collective-permute-start.6
  10.1 5.1 %collective-permute-done.2.refs_13_ = bf16[32,1408]{1,0:T(8,128)(2,1)S(1)} collective-permute-done((bf16[32,1408]{1,0:T(8,128)(2,1)S(1)}, bf16[32,1408]{1,0:T(8,128)(2,1)S(1)}, u32[]{:S(2)}, u32[]{:S(2)}) %collective-permute-start.2) | collective-permute-done | bytes 90144 | tf_op jit(solution)/shard_map/ppermute | solution.py:270
  15.2 0.0 collective-permute-start.5
  15.2 0.0 collective-permute-done.1.refs_12_
  15.2 0.5 %collective-permute-start.4 = (bf16[32,1408]{1,0:T(8,128)(2,1)S(1)}, bf16[32,1408]{1,0:T(8,128)(2,1)S(1)}, u32[]{:S(2)}, u32[]{:S(2)}) collective-permute-start(bf16[32,1408]{1,0:T(8,128)(2,1)S(1)} %collective-permute-done.1.refs_12_), channel_id=1, source_target_pairs={{0,1},{1,0},{2,3},{3,2},{4,5},{5,4},{6,7},{7,6},{8,9},{9,8},{10,11... | collective-permute-start | bytes 270344 | tf_op jit(solution)/shard_map/ppermute | solution.py:270
  15.7 0.0 collective-permute-start
  15.7 0.0 copy-start
  15.8 3.0 %meanwhile.1 = (bf16[1280,640]{1,0:T(8,128)(2,1)S(1)}, bf16[1280,640]{1,0:T(8,128)(2,1)S(1)}, bf16[1280,640]{1,0:T(8,128)(2,1)S(1)}, bf16[640,1280]{1,0:T(8,128)...) custom-call(bf16[64,1280]{1,0:T(8,128)(2,1)S(1)} %get-tuple-element., ...), custom_call_target="tpu_custom_call" | custom-call | tf_op jit(solution)/shard_map/meanwhile/pallas_call | solution.py:322
  18.7 0.0 collective-permute-done.refs_11_
  18.7 0.0 collective-permute-done.6.refs_17_
  18.8 0.0 collective-permute-done.5.refs_16_
  18.8 0.0 collective-permute-done.4.refs_15_
  18.8 0.0 copy-done
  18.8 3.7 %first_block.1 = (bf16[128,640]{1,0:T(8,128)(2,1)S(1)}, bf16[128,640]{1,0:T(8,128)(2,1)S(1)}, bf16[256,640]{1,0:T(8,128)(2,1)S(1)}, bf16[256,640]{1,0:T(8,128)(2,1)S(1)}, f32[8,1280]{1,0:T(8,128)S(1)}) custom-call(s32[4,16]{1,0:T(4,128)S(1)} %copy-done, bf16[256,1280]{1,0:T(8,128)(2,1)S(1)} %get-tuple-element.24.refs_1_, ...), custom_call_target="tpu_custom_call" | custom-call | tf_op jit(solution)/shard_map/first_block/pallas_call | solution.py:342
  22.5 1.5 %collective-permute-start.7 = (bf16[128,640]{1,0:T(8,128)(2,1)S(1)}, bf16[128,640]{1,0:T(8,128)(2,1)S(1)}, u32[]{:S(2)}, u32[]{:S(2)}) collective-permute-start(bf16[128,640]{1,0:T(8,128)(2,1)S(1)} %get-tuple-element.37), channel_id=1, source_target_pairs={{0,2},{2,0},{1,3},{3,1},{4,6},{6,4},{5,7},{7,5},{8,10},{10,8},{9,1... | collective-permute-start | bytes 491528 | tf_op jit(solution)/shard_map/ppermute | solution.py:270
  24.1 2.6 %second_block.1 = (bf16[128,640]{1,0:T(8,128)(2,1)S(1)}, bf16[128,640]{1,0:T(8,128)(2,1)S(1)}) custom-call(s32[4,16]{1,0:T(4,128)S(1)} %copy-done, bf16[256,1280]{1,0:T(8,128)(2,1)S(1)} %get-tuple-element.24.refs_1_, f32[20,128]{1,0:T(8,128)S(1)} %get-tuple-element.28.refs_4_.refs_2_, f32[10,128]{1,0:T(8,128)S(1)} %get-tuple-element.29.refs_5_.refs_3_, ...), custom_call_target="tpu_custom_call" | custom-call | tf_op jit(solution)/shard_map/second_block/pallas_call | solution.py:356
  26.7 0.6 %collective-permute-start.8 = (bf16[128,640]{1,0:T(8,128)(2,1)S(1)}, bf16[128,640]{1,0:T(8,128)(2,1)S(1)}, u32[]{:S(2)}, u32[]{:S(2)}) collective-permute-start(bf16[128,640]{1,0:T(8,128)(2,1)S(1)} %get-tuple-element.42), channel_id=1, source_target_pairs={{0,2},{2,0},{1,3},{3,1},{4,6},{6,4},{5,7},{7,5},{8,10},{10,8},{9,1... | collective-permute-start | bytes 491528 | tf_op jit(solution)/shard_map/ppermute | solution.py:270
  27.3 1.9 %collective-permute-done.7.got_a = bf16[128,640]{1,0:T(8,128)(2,1)S(1)} collective-permute-done((bf16[128,640]{1,0:T(8,128)(2,1)S(1)}, bf16[128,640]{1,0:T(8,128)(2,1)S(1)}, u32[]{:S(2)}, u32[]{:S(2)}) %collective-permute-start.7) | collective-permute-done | bytes 163872 | tf_op jit(solution)/shard_map/ppermute | solution.py:270
  29.2 3.9 %collective-permute-done.8.got_b = bf16[128,640]{1,0:T(8,128)(2,1)S(1)} collective-permute-done((bf16[128,640]{1,0:T(8,128)(2,1)S(1)}, bf16[128,640]{1,0:T(8,128)(2,1)S(1)}, u32[]{:S(2)}, u32[]{:S(2)}) %collective-permute-start.8) | collective-permute-done | bytes 163872 | tf_op jit(solution)/shard_map/ppermute | solution.py:270
  33.1 0.8 %add_up.1 = bf16[256,640]{1,0:T(8,128)(2,1)} custom-call(bf16[128,640]{1,0:T(8,128)(2,1)S(1)} %get-tuple-element.36.own_a, bf16[128,640]{1,0:T(8,128)(2,1)S(1)} %collective-permute-done.7.got_a, bf16[128,640]{1,0:T(8,128)(2,1)S(1)} %get-tuple-element.41.own_b, bf16[128,640]{1,0:T(8,128)(2,1)S(1)} %collective-permute-done.8.got_b), custom_call_target="tpu_custom_call" | custom-call | tf_op jit(solution)/shard_map/add_up/pallas_call | solution.py:367
Async XLA Ops:
  2.0 8.1 %collective-permute-start.3 = (bf16[32,1408]{1,0:T(8,128)(2,1)S(1)}, bf16[32,1408]{1,0:T(8,128)(2,1)S(1)}, u32[]{:S(2)}, u32[]{:S(2)}) collective-permute-start(bf16[32,1408]{1,0:T(8,128)(2,1)S(1)} %get-tuple-element.35), channel_id=1, source_target_pairs={{0,12},{4,0},{8,4},{12,8},{1,13},{5,1},{9,5},{13,9},{2,14},{6,2},{... | collective-permute-start | bytes 270344 | tf_op jit(solution)/shard_map/ppermute | solution.py:270
  7.1 8.1 %collective-permute-start.2 = (bf16[32,1408]{1,0:T(8,128)(2,1)S(1)}, bf16[32,1408]{1,0:T(8,128)(2,1)S(1)}, u32[]{:S(2)}, u32[]{:S(2)}) collective-permute-start(bf16[32,1408]{1,0:T(8,128)(2,1)S(1)} %get-tuple-element.35), channel_id=1, source_target_pairs={{0,8},{4,12},{8,0},{12,4},{1,9},{5,13},{9,1},{13,5},{2,10},{6,14},... | collective-permute-start | bytes 270344 | tf_op jit(solution)/shard_map/ppermute | solution.py:270
  7.1 8.1 %collective-permute-start.1 = (bf16[32,1408]{1,0:T(8,128)(2,1)S(1)}, bf16[32,1408]{1,0:T(8,128)(2,1)S(1)}, u32[]{:S(2)}, u32[]{:S(2)}) collective-permute-start(bf16[32,1408]{1,0:T(8,128)(2,1)S(1)} %get-tuple-element.35), channel_id=1, source_target_pairs={{0,4},{4,8},{8,12},{12,0},{1,5},{5,9},{9,13},{13,1},{2,6},{6,10},{... | collective-permute-start | bytes 270344 | tf_op jit(solution)/shard_map/ppermute | solution.py:270
  10.1 8.7 %collective-permute-start.6 = (bf16[32,1408]{1,0:T(8,128)(2,1)S(1)}, bf16[32,1408]{1,0:T(8,128)(2,1)S(1)}, u32[]{:S(2)}, u32[]{:S(2)}) collective-permute-start(bf16[32,1408]{1,0:T(8,128)(2,1)S(1)} %collective-permute-done.3.refs_14_), channel_id=1, source_target_pairs={{0,1},{1,0},{2,3},{3,2},{4,5},{5,4},{6,7},{7,6},{8,9},{9,8},{10,11... | collective-permute-start | bytes 270344 | tf_op jit(solution)/shard_map/ppermute | solution.py:270
  15.2 3.5 %collective-permute-start.5 = (bf16[32,1408]{1,0:T(8,128)(2,1)S(1)}, bf16[32,1408]{1,0:T(8,128)(2,1)S(1)}, u32[]{:S(2)}, u32[]{:S(2)}) collective-permute-start(bf16[32,1408]{1,0:T(8,128)(2,1)S(1)} %collective-permute-done.2.refs_13_), channel_id=1, source_target_pairs={{0,1},{1,0},{2,3},{3,2},{4,5},{5,4},{6,7},{7,6},{8,9},{9,8},{10,11... | collective-permute-start | bytes 270344 | tf_op jit(solution)/shard_map/ppermute | solution.py:270
  15.2 3.5 %collective-permute-start.4 = (bf16[32,1408]{1,0:T(8,128)(2,1)S(1)}, bf16[32,1408]{1,0:T(8,128)(2,1)S(1)}, u32[]{:S(2)}, u32[]{:S(2)}) collective-permute-start(bf16[32,1408]{1,0:T(8,128)(2,1)S(1)} %collective-permute-done.1.refs_12_), channel_id=1, source_target_pairs={{0,1},{1,0},{2,3},{3,2},{4,5},{5,4},{6,7},{7,6},{8,9},{9,8},{10,11... | collective-permute-start | bytes 270344 | tf_op jit(solution)/shard_map/ppermute | solution.py:270
  15.7 3.0 %collective-permute-start = (bf16[32,128]{1,0:T(8,128)(2,1)S(1)}, bf16[32,128]{1,0:T(8,128)(2,1)S(1)}, u32[]{:S(2)}, u32[]{:S(2)}) collective-permute-start(bf16[32,128]{1,0:T(8,128)(2,1)S(1)} %get-tuple-element.34.refs_10_), channel_id=1, source_target_pairs={{0,1},{1,0},{2,3},{3,2},{4,5},{5,4},{6,7},{7,6},{8,9},{9,8},{10,11... | collective-permute-start | bytes 24584 | tf_op jit(solution)/shard_map/ppermute | solution.py:270
  15.7 3.0 %copy-start = (s32[4,16]{1,0:T(4,128)S(1)}, s32[4,16]{1,0:T(4,128)}, u32[]{:S(2)}) copy-start(s32[4,16]{1,0:T(4,128)} %refs_0_.5) | copy-start | bytes 772
  22.5 6.7 %collective-permute-start.7 = (bf16[128,640]{1,0:T(8,128)(2,1)S(1)}, bf16[128,640]{1,0:T(8,128)(2,1)S(1)}, u32[]{:S(2)}, u32[]{:S(2)}) collective-permute-start(bf16[128,640]{1,0:T(8,128)(2,1)S(1)} %get-tuple-element.37), channel_id=1, source_target_pairs={{0,2},{2,0},{1,3},{3,1},{4,6},{6,4},{5,7},{7,5},{8,10},{10,8},{9,1... | collective-permute-start | bytes 491528 | tf_op jit(solution)/shard_map/ppermute | solution.py:270
  26.7 6.4 %collective-permute-start.8 = (bf16[128,640]{1,0:T(8,128)(2,1)S(1)}, bf16[128,640]{1,0:T(8,128)(2,1)S(1)}, u32[]{:S(2)}, u32[]{:S(2)}) collective-permute-start(bf16[128,640]{1,0:T(8,128)(2,1)S(1)} %get-tuple-element.42), channel_id=1, source_target_pairs={{0,2},{2,0},{1,3},{3,1},{4,6},{6,4},{5,7},{7,5},{8,10},{10,8},{9,1... | collective-permute-start | bytes 491528 | tf_op jit(solution)/shard_map/ppermute | solution.py:270

commit v3 on v2

--- a/solution.py
+++ b/solution.py
@@ -27,10 +27,11 @@
 
 def group_of_channel(channels):
     size = channels // GROUPS
-    row = lax.broadcasted_iota(jnp.int32, (LANES, channels), 0)
-    col = lax.broadcasted_iota(jnp.int32, (LANES, channels), 1)
+    row = lax.broadcasted_iota(jnp.int32, (GROUPS, channels), 0)
+    col = lax.broadcasted_iota(jnp.int32, (GROUPS, channels), 1)
     first = row * size
-    return jnp.where((col >= first) & (col < first + size), 1.0, 0.0).astype(BF16)
+    some = jnp.where((col >= first) & (col < first + size), 1.0, 0.0).astype(BF16)
+    return jnp.concatenate([some, jnp.zeros((LANES - GROUPS, channels), BF16)], axis=0)
 
 
 def exact_dot(v, member, dims):
@@ -62,11 +63,15 @@
     means, squares = [], []
     for b in range(2):
         loads[b].wait()
-        x = canvas_ref[b * n : (b + 1) * n, :].astype(F32)
-        mean = jnp.sum(x, axis=0, keepdims=True) * (1.0 / n)
-        c = x - mean
-        means.append(mean)
-        squares.append(jnp.sum(c * c, axis=0, keepdims=True))
+        mean_parts, square_parts = [], []
+        for j in range(channels // LANES):
+            x = canvas_ref[b * n : (b + 1) * n, j * LANES : (j + 1) * LANES].astype(F32)
+            mean = jnp.sum(x, axis=0, keepdims=True) * (1.0 / n)
+            c = x - mean
+            mean_parts.append(mean)
+            square_parts.append(jnp.sum(c * c, axis=0, keepdims=True))
+        means.append(jnp.concatenate(mean_parts, axis=1))
+        squares.append(jnp.concatenate(square_parts, axis=1))
     member = group_of_channel(channels)
     mean_g = exact_dot(rows_of({0: means[0], 1: means[1]}, channels), member, NT) * (1.0 / size)
     back = exact_dot(mean_g, member, (((1,), (0,)), ((), ())))
@@ -152,21 +157,16 @@
         send_ref[...] = term.astype(BF16)
 
 
-def merged_stats(stats, tile, n_tile, count, member):
-    live = {}
-    for o in range(-2, 3):
-        ok = (tile + o >= 0) & (tile + o < n_tile)
-        gate = jnp.where(ok, 1.0, 0.0).astype(F32)
-        live[o] = [v * gate for v in stats[o]]
+def merged_stats(stats, count, member):
     rows = {}
     for i, o in enumerate((-1, 0, 1)):
         blocks = []
         for s in range(len(stats[0])):
             blocks += [
-                (live[o - 1][s][1:2], live[o - 1][s][3:4]),
-                (live[o][s][0:1], live[o][s][2:3]),
-                (live[o][s][1:2], live[o][s][3:4]),
-                (live[o + 1][s][0:1], live[o + 1][s][2:3]),
+                (stats[o - 1][s][1:2], stats[o - 1][s][3:4]),
+                (stats[o][s][0:1], stats[o][s][2:3]),
+                (stats[o][s][1:2], stats[o][s][3:4]),
+                (stats[o + 1][s][0:1], stats[o + 1][s][2:3]),
             ]
         mean = sum(m for m, _ in blocks) * (1.0 / len(blocks))
         m2 = sum(q for _, q in blocks) + count * sum((m - mean) * (m - mean) for m, _ in blocks)
@@ -188,10 +188,13 @@
 def fill_normed(canvas_ref, rows, affine, normed_ref, order):
     chan, gain, shift = affine
     n = normed_ref.shape[0] // 2
-    x = canvas_ref[rows, :].astype(F32)
-    for i, o in enumerate(order):
-        mean, rstd = chan[o + 1 : o + 2], chan[o + 4 : o + 5]
-        normed_ref[i * n : (i + 1) * n, :] = ((x - mean) * (rstd * gain) + shift).astype(BF16)
+    for j in range(canvas_ref.shape[1] // LANES):
+        cols = slice(j * LANES, (j + 1) * LANES)
+        x = canvas_ref[rows, cols].astype(F32)
+        for i, o in enumerate(order):
+            mean, rstd = chan[o + 1 : o + 2, cols], chan[o + 4 : o + 5, cols]
+            normed = (x - mean) * (rstd * gain[:, cols]) + shift[:, cols]
+            normed_ref[i * n : (i + 1) * n, cols] = normed.astype(BF16)
 
 
 def first_block(n_tile, split, count, columns, *refs):
@@ -214,11 +217,17 @@
         return v[0:8] + v[8:16] + v[16:24]
 
     full, tail = slice(0, LANES), slice(channels, channels + LANES)
-    stats = {0: [stat(st_ref, full), stat(st_peer_ref, full)]}
-    for o in (-2, -1, 1, 2):
-        k = (-o) % n_tile
-        stats[o] = [stat(near[k - 1], tail), stat(far[k - 1], tail)] if k else stats[0]
-    chan = merged_stats(stats, tile, n_tile, float(count), group_of_channel(channels))
+    held = {0: [stat(st_ref, full), stat(st_peer_ref, full)]}
+    for k in range(1, n_tile):
+        if in_pairs(n_tile) or min(k, n_tile - k) <= 2:
+            held[k] = [stat(near[k - 1], tail), stat(far[k - 1], tail)]
+    stats = {}
+    for o in range(-2, 3):
+        stats[o] = [jnp.zeros_like(v) for v in held[0]]
+        for k, got in held.items():
+            hit = jnp.where(partner(tile, n_tile, k) == tile + o, 1.0, 0.0).astype(F32)
+            stats[o] = [a + v * hit for a, v in zip(stats[o], got)]
+    chan = merged_stats(stats, float(count), group_of_channel(channels))
     gain, shift = gain_and_shift(temb_ref, gain_ref)
     n = normed_ref.shape[0] // 2
     fill_normed(canvas_ref, slice(0, n), (chan, gain, shift), normed_ref, (0, -1))
@@ -267,7 +276,15 @@
 
 def shifted(value, axis, step):
     count = lax.axis_size(axis)
-    return lax.ppermute(value, axis, [(i, (i + step) % count) for i in range(count)])
+    return lax.ppermute(value, axis, [(partner(i, count, step), i) for i in range(count)])
+
+
+def in_pairs(count):
+    return count in (1, 2, 4)
+
+
+def partner(i, count, step):
+    return i ^ step if in_pairs(count) else (i - step) % count
 
 
 def on_device(canvas, thumb, ramps, t_embed, norm_gain, w_query, w_key, w_value, w_out):
@@ -327,7 +344,7 @@
     else:
         every = lax.all_gather(payload, "tile", axis=0)
         me = lax.axis_index("tile")
-        near = [lax.dynamic_index_in_dim(every, (me - k) % n_tile, 0, False) for k in range(1, n_tile)]
+        near = [lax.dynamic_index_in_dim(every, partner(me, n_tile, k), 0, False) for k in range(1, n_tile)]
     st_peer = shifted(st, "sub", 1)
     far = [shifted(v, "sub", 1) for v in near]
 
@@ -353,7 +370,7 @@
     )
     first, (keys, values, chan) = outs[: len(parts)], outs[len(parts) :]
     got_a = shifted(first[0], "chan", 1) if split else None
-    second = pl.pallas_call(
+    more = pl.pallas_call(
         functools.partial(second_block, n_tile, split, columns),
         out_shape=parts,
         in_specs=[smem] + [vmem] * 8,
@@ -361,7 +378,8 @@
         scratch_shapes=work,
         compiler_params=pltpu.CompilerParams(vmem_limit_bytes=20 << 20),
         name="second_block",
-    )(ramps, x, temb, gain, w_query, w_out, *resident(keys, values, chan))
+    )
+    second = more(ramps, x, temb, gain, w_query, w_out, *resident(keys, values, chan))
     if split:
         got_b = shifted(second[0], "chan", 1)
         out = pl.pallas_call(

time: 34 us -> 33.2 us (0.976)
  no operation moved by 1% of the time
where the time goes in v3:
time: 33.2 us; the launch traced here: 33.1 us
  waiting for transfers between devices  12.7 us (38%)
  Pallas kernels  11.8 us (36%)
  starting transfers between devices  8.46 us (25%)
    ppermute x9, waiting for transfers between devices, shifted(): lax.ppermute(value, axis, [(partner(i, count, step), i) for i in range(co...  12.7 us
    ppermute x9, starting transfers between devices, shifted(): lax.ppermute(value, axis, [(partner(i, count, step), i) for i in range(co...  8.46 us
    pallas_call x1, Pallas kernels, on_device(): pl.pallas_call(functools.partial(first_block, n_tile, split, count, colum...  3.68 us
    pallas_call x1, Pallas kernels, on_device(): *brought, k_own, v_own = bring(thumb, *in_hbm(*brought))  2.98 us
    pallas_call x1, Pallas kernels, on_device(): more(ramps, x, temb, gain, w_query, w_out, *resident(keys, values, chan))  2.63 us
    pallas_call x1, Pallas kernels, on_device(): pl.pallas_call(local_stats, out_shape=(pltpu.VMEM((half, channels + LANES...  1.73 us
    pallas_call x1, Pallas kernels, on_device(): pl.pallas_call(add_up, out_shape=jax.ShapeDtypeStruct((rows, channels //...  0.81 us
  transfers between devices with their start and end apart: 9, of which 4 were waited for; matrix products, arithmetic and copies ran while one was open for 0% of the time, Pallas kernels for 17%

profile of v3, /device:TPU:0, one launch (start us, length us, event | category | flops | bytes accessed | tf_op | source)
XLA Modules:
  0.0 33.1 jit_solution(7327357793126158562)
XLA Ops:
  0.0 1.7 %local_stats.1 = (bf16[32,1408]{1,0:T(8,128)(2,1)S(1)}, bf16[32,128]{1,0:T(8,128)(2,1)S(1)}, bf16[256,1280]{1,0:T(8,128)(2,1)S(1)}, bf16[64,1280]{1,0:T(8,128)(2,1)S(1)}) custom-call(bf16[256,1280]{1,0:T(8,128)(2,1)} %bitcast.4, bf16[64,1280]{1,0:T(8,128)(2,1)} %thumb_hbm.1), custom_call_target="tpu_custom_call" | custom-call | tf_op jit(solution)/shard_map/local_stats/pallas_call | solution.py:311
  1.7 5.1 %collective-permute-start.3 = (bf16[32,1408]{1,0:T(8,128)(2,1)S(1)}, bf16[32,1408]{1,0:T(8,128)(2,1)S(1)}, u32[]{:S(2)}, u32[]{:S(2)}) collective-permute-start(bf16[32,1408]{1,0:T(8,128)(2,1)S(1)} %get-tuple-element.35), channel_id=1, source_target_pairs={{12,0},{8,4},{4,8},{0,12},{13,1},{9,5},{5,9},{1,13},{14,2},{10,6},... | collective-permute-start | bytes 270344 | tf_op jit(solution)/shard_map/ppermute | solution.py:279
  6.9 0.0 collective-permute-start.2
  6.9 0.6 %collective-permute-start.1 = (bf16[32,1408]{1,0:T(8,128)(2,1)S(1)}, bf16[32,1408]{1,0:T(8,128)(2,1)S(1)}, u32[]{:S(2)}, u32[]{:S(2)}) collective-permute-start(bf16[32,1408]{1,0:T(8,128)(2,1)S(1)} %get-tuple-element.35), channel_id=1, source_target_pairs={{4,0},{0,4},{12,8},{8,12},{5,1},{1,5},{13,9},{9,13},{6,2},{2,6},{1... | collective-permute-start | bytes 270344 | tf_op jit(solution)/shard_map/ppermute | solution.py:279
  7.5 2.7 %collective-permute-done.3.refs_14_ = bf16[32,1408]{1,0:T(8,128)(2,1)S(1)} collective-permute-done((bf16[32,1408]{1,0:T(8,128)(2,1)S(1)}, bf16[32,1408]{1,0:T(8,128)(2,1)S(1)}, u32[]{:S(2)}, u32[]{:S(2)}) %collective-permute-start.3) | collective-permute-done | bytes 90144 | tf_op jit(solution)/shard_map/ppermute | solution.py:279
  10.2 0.0 collective-permute-start.6
  10.2 4.2 %collective-permute-done.2.refs_13_ = bf16[32,1408]{1,0:T(8,128)(2,1)S(1)} collective-permute-done((bf16[32,1408]{1,0:T(8,128)(2,1)S(1)}, bf16[32,1408]{1,0:T(8,128)(2,1)S(1)}, u32[]{:S(2)}, u32[]{:S(2)}) %collective-permute-start.2) | collective-permute-done | bytes 90144 | tf_op jit(solution)/shard_map/ppermute | solution.py:279
  14.4 0.0 collective-permute-start.5
  14.5 0.0 collective-permute-done.1.refs_12_
  14.5 0.5 %collective-permute-start.4 = (bf16[32,1408]{1,0:T(8,128)(2,1)S(1)}, bf16[32,1408]{1,0:T(8,128)(2,1)S(1)}, u32[]{:S(2)}, u32[]{:S(2)}) collective-permute-start(bf16[32,1408]{1,0:T(8,128)(2,1)S(1)} %collective-permute-done.1.refs_12_), channel_id=1, source_target_pairs={{1,0},{0,1},{3,2},{2,3},{5,4},{4,5},{7,6},{6,7},{9,8},{8,9},{11,10... | collective-permute-start | bytes 270344 | tf_op jit(solution)/shard_map/ppermute | solution.py:279
  15.0 0.0 collective-permute-start
  15.0 0.0 copy-start
  15.0 3.0 %meanwhile.1 = (bf16[1280,640]{1,0:T(8,128)(2,1)S(1)}, bf16[1280,640]{1,0:T(8,128)(2,1)S(1)}, bf16[1280,640]{1,0:T(8,128)(2,1)S(1)}, bf16[640,1280]{1,0:T(8,128)...) custom-call(bf16[64,1280]{1,0:T(8,128)(2,1)S(1)} %get-tuple-element., ...), custom_call_target="tpu_custom_call" | custom-call | tf_op jit(solution)/shard_map/meanwhile/pallas_call | solution.py:339
  18.0 0.0 collective-permute-done.refs_11_
  18.0 0.0 collective-permute-done.6.refs_17_
  18.0 0.0 collective-permute-done.5.refs_16_
  18.0 0.0 collective-permute-done.4.refs_15_
  18.0 0.0 copy-done
  18.0 3.7 %first_block.1 = (bf16[128,640]{1,0:T(8,128)(2,1)S(1)}, bf16[128,640]{1,0:T(8,128)(2,1)S(1)}, bf16[256,640]{1,0:T(8,128)(2,1)S(1)}, bf16[256,640]{1,0:T(8,128)(2,1)S(1)}, f32[8,1280]{1,0:T(8,128)S(1)}) custom-call(s32[4,16]{1,0:T(4,128)S(1)} %copy-done, bf16[256,1280]{1,0:T(8,128)(2,1)S(1)} %get-tuple-element.24.refs_1_, ...), custom_call_target="tpu_custom_call" | custom-call | tf_op jit(solution)/shard_map/first_block/pallas_call | solution.py:359
  21.7 1.6 %collective-permute-start.7 = (bf16[128,640]{1,0:T(8,128)(2,1)S(1)}, bf16[128,640]{1,0:T(8,128)(2,1)S(1)}, u32[]{:S(2)}, u32[]{:S(2)}) collective-permute-start(bf16[128,640]{1,0:T(8,128)(2,1)S(1)} %get-tuple-element.37), channel_id=1, source_target_pairs={{2,0},{0,2},{3,1},{1,3},{6,4},{4,6},{7,5},{5,7},{10,8},{8,10},{11,... | collective-permute-start | bytes 491528 | tf_op jit(solution)/shard_map/ppermute | solution.py:279
  23.3 2.6 %second_block.1 = (bf16[128,640]{1,0:T(8,128)(2,1)S(1)}, bf16[128,640]{1,0:T(8,128)(2,1)S(1)}) custom-call(s32[4,16]{1,0:T(4,128)S(1)} %copy-done, bf16[256,1280]{1,0:T(8,128)(2,1)S(1)} %get-tuple-element.24.refs_1_, f32[20,128]{1,0:T(8,128)S(1)} %get-tuple-element.28.refs_4_.refs_2_, f32[10,128]{1,0:T(8,128)S(1)} %get-tuple-element.29.refs_5_.refs_3_, ...), custom_call_target="tpu_custom_call" | custom-call | tf_op jit(solution)/shard_map/second_block/pallas_call | solution.py:382
  25.9 0.6 %collective-permute-start.8 = (bf16[128,640]{1,0:T(8,128)(2,1)S(1)}, bf16[128,640]{1,0:T(8,128)(2,1)S(1)}, u32[]{:S(2)}, u32[]{:S(2)}) collective-permute-start(bf16[128,640]{1,0:T(8,128)(2,1)S(1)} %get-tuple-element.42), channel_id=1, source_target_pairs={{2,0},{0,2},{3,1},{1,3},{6,4},{4,6},{7,5},{5,7},{10,8},{8,10},{11,... | collective-permute-start | bytes 491528 | tf_op jit(solution)/shard_map/ppermute | solution.py:279
  26.5 1.9 %collective-permute-done.7.got_a = bf16[128,640]{1,0:T(8,128)(2,1)S(1)} collective-permute-done((bf16[128,640]{1,0:T(8,128)(2,1)S(1)}, bf16[128,640]{1,0:T(8,128)(2,1)S(1)}, u32[]{:S(2)}, u32[]{:S(2)}) %collective-permute-start.7) | collective-permute-done | bytes 163872 | tf_op jit(solution)/shard_map/ppermute | solution.py:279
  28.4 3.9 %collective-permute-done.8.got_b = bf16[128,640]{1,0:T(8,128)(2,1)S(1)} collective-permute-done((bf16[128,640]{1,0:T(8,128)(2,1)S(1)}, bf16[128,640]{1,0:T(8,128)(2,1)S(1)}, u32[]{:S(2)}, u32[]{:S(2)}) %collective-permute-start.8) | collective-permute-done | bytes 163872 | tf_op jit(solution)/shard_map/ppermute | solution.py:279
  32.3 0.8 %add_up.1 = bf16[256,640]{1,0:T(8,128)(2,1)} custom-call(bf16[128,640]{1,0:T(8,128)(2,1)S(1)} %get-tuple-element.36.own_a, bf16[128,640]{1,0:T(8,128)(2,1)S(1)} %collective-permute-done.7.got_a, bf16[128,640]{1,0:T(8,128)(2,1)S(1)} %get-tuple-element.41.own_b, bf16[128,640]{1,0:T(8,128)(2,1)S(1)} %collective-permute-done.8.got_b), custom_call_target="tpu_custom_call" | custom-call | tf_op jit(solution)/shard_map/add_up/pallas_call | solution.py:385
Async XLA Ops:
  1.7 8.5 %collective-permute-start.3 = (bf16[32,1408]{1,0:T(8,128)(2,1)S(1)}, bf16[32,1408]{1,0:T(8,128)(2,1)S(1)}, u32[]{:S(2)}, u32[]{:S(2)}) collective-permute-start(bf16[32,1408]{1,0:T(8,128)(2,1)S(1)} %get-tuple-element.35), channel_id=1, source_target_pairs={{12,0},{8,4},{4,8},{0,12},{13,1},{9,5},{5,9},{1,13},{14,2},{10,6},... | collective-permute-start | bytes 270344 | tf_op jit(solution)/shard_map/ppermute | solution.py:279
  6.9 7.6 %collective-permute-start.2 = (bf16[32,1408]{1,0:T(8,128)(2,1)S(1)}, bf16[32,1408]{1,0:T(8,128)(2,1)S(1)}, u32[]{:S(2)}, u32[]{:S(2)}) collective-permute-start(bf16[32,1408]{1,0:T(8,128)(2,1)S(1)} %get-tuple-element.35), channel_id=1, source_target_pairs={{8,0},{12,4},{0,8},{4,12},{9,1},{13,5},{1,9},{5,13},{10,2},{14,6},... | collective-permute-start | bytes 270344 | tf_op jit(solution)/shard_map/ppermute | solution.py:279
  6.9 7.6 %collective-permute-start.1 = (bf16[32,1408]{1,0:T(8,128)(2,1)S(1)}, bf16[32,1408]{1,0:T(8,128)(2,1)S(1)}, u32[]{:S(2)}, u32[]{:S(2)}) collective-permute-start(bf16[32,1408]{1,0:T(8,128)(2,1)S(1)} %get-tuple-element.35), channel_id=1, source_target_pairs={{4,0},{0,4},{12,8},{8,12},{5,1},{1,5},{13,9},{9,13},{6,2},{2,6},{1... | collective-permute-start | bytes 270344 | tf_op jit(solution)/shard_map/ppermute | solution.py:279
  10.2 7.7 %collective-permute-start.6 = (bf16[32,1408]{1,0:T(8,128)(2,1)S(1)}, bf16[32,1408]{1,0:T(8,128)(2,1)S(1)}, u32[]{:S(2)}, u32[]{:S(2)}) collective-permute-start(bf16[32,1408]{1,0:T(8,128)(2,1)S(1)} %collective-permute-done.3.refs_14_), channel_id=1, source_target_pairs={{1,0},{0,1},{3,2},{2,3},{5,4},{4,5},{7,6},{6,7},{9,8},{8,9},{11,10... | collective-permute-start | bytes 270344 | tf_op jit(solution)/shard_map/ppermute | solution.py:279
  14.4 3.5 %collective-permute-start.5 = (bf16[32,1408]{1,0:T(8,128)(2,1)S(1)}, bf16[32,1408]{1,0:T(8,128)(2,1)S(1)}, u32[]{:S(2)}, u32[]{:S(2)}) collective-permute-start(bf16[32,1408]{1,0:T(8,128)(2,1)S(1)} %collective-permute-done.2.refs_13_), channel_id=1, source_target_pairs={{1,0},{0,1},{3,2},{2,3},{5,4},{4,5},{7,6},{6,7},{9,8},{8,9},{11,10... | collective-permute-start | bytes 270344 | tf_op jit(solution)/shard_map/ppermute | solution.py:279
  14.5 3.5 %collective-permute-start.4 = (bf16[32,1408]{1,0:T(8,128)(2,1)S(1)}, bf16[32,1408]{1,0:T(8,128)(2,1)S(1)}, u32[]{:S(2)}, u32[]{:S(2)}) collective-permute-start(bf16[32,1408]{1,0:T(8,128)(2,1)S(1)} %collective-permute-done.1.refs_12_), channel_id=1, source_target_pairs={{1,0},{0,1},{3,2},{2,3},{5,4},{4,5},{7,6},{6,7},{9,8},{8,9},{11,10... | collective-permute-start | bytes 270344 | tf_op jit(solution)/shard_map/ppermute | solution.py:279
  15.0 3.0 %collective-permute-start = (bf16[32,128]{1,0:T(8,128)(2,1)S(1)}, bf16[32,128]{1,0:T(8,128)(2,1)S(1)}, u32[]{:S(2)}, u32[]{:S(2)}) collective-permute-start(bf16[32,128]{1,0:T(8,128)(2,1)S(1)} %get-tuple-element.34.refs_10_), channel_id=1, source_target_pairs={{1,0},{0,1},{3,2},{2,3},{5,4},{4,5},{7,6},{6,7},{9,8},{8,9},{11,10... | collective-permute-start | bytes 24584 | tf_op jit(solution)/shard_map/ppermute | solution.py:279
  15.0 3.0 %copy-start = (s32[4,16]{1,0:T(4,128)S(1)}, s32[4,16]{1,0:T(4,128)}, u32[]{:S(2)}) copy-start(s32[4,16]{1,0:T(4,128)} %refs_0_.5) | copy-start | bytes 772
  21.7 6.7 %collective-permute-start.7 = (bf16[128,640]{1,0:T(8,128)(2,1)S(1)}, bf16[128,640]{1,0:T(8,128)(2,1)S(1)}, u32[]{:S(2)}, u32[]{:S(2)}) collective-permute-start(bf16[128,640]{1,0:T(8,128)(2,1)S(1)} %get-tuple-element.37), channel_id=1, source_target_pairs={{2,0},{0,2},{3,1},{1,3},{6,4},{4,6},{7,5},{5,7},{10,8},{8,10},{11,... | collective-permute-start | bytes 491528 | tf_op jit(solution)/shard_map/ppermute | solution.py:279
  25.9 6.4 %collective-permute-start.8 = (bf16[128,640]{1,0:T(8,128)(2,1)S(1)}, bf16[128,640]{1,0:T(8,128)(2,1)S(1)}, u32[]{:S(2)}, u32[]{:S(2)}) collective-permute-start(bf16[128,640]{1,0:T(8,128)(2,1)S(1)} %get-tuple-element.42), channel_id=1, source_target_pairs={{2,0},{0,2},{3,1},{1,3},{6,4},{4,6},{7,5},{5,7},{10,8},{8,10},{11,... | collective-permute-start | bytes 491528 | tf_op jit(solution)/shard_map/ppermute | solution.py:279

commit v4 on v3

--- a/solution.py
+++ b/solution.py
@@ -15,6 +15,7 @@
 EPS = 1e-05
 F32 = jnp.float32
 BF16 = jnp.bfloat16
+CHUNKS = (4, 4)
 NT = (((1,), (1,)), ((), ()))
 
 
@@ -50,7 +51,7 @@
 
 def local_stats(canvas_hbm, thumb_hbm, pay_ref, st_ref, canvas_ref, thumb_ref, sems):
     channels = canvas_ref.shape[1]
-    half = pay_ref.shape[0]
+    half = (pay_ref.shape[0] - 16) * LANES // channels
     n = canvas_ref.shape[0] // 2
     size = channels // GROUPS
     loads = []
@@ -60,6 +61,7 @@
     loads.append(pltpu.make_async_copy(thumb_hbm, thumb_ref, sems.at[2]))
     for load in loads:
         load.start()
+    member = group_of_channel(channels)
     means, squares = [], []
     for b in range(2):
         loads[b].wait()
@@ -72,7 +74,6 @@
             square_parts.append(jnp.sum(c * c, axis=0, keepdims=True))
         means.append(jnp.concatenate(mean_parts, axis=1))
         squares.append(jnp.concatenate(square_parts, axis=1))
-    member = group_of_channel(channels)
     mean_g = exact_dot(rows_of({0: means[0], 1: means[1]}, channels), member, NT) * (1.0 / size)
     back = exact_dot(mean_g, member, (((1,), (0,)), ((), ())))
     tot = []
@@ -80,14 +81,15 @@
         diff = means[b] - back[b : b + 1]
         tot.append(squares[b] + n * (diff * diff))
     m2_g = exact_dot(rows_of({2: tot[0], 3: tot[1]}, channels), member, NT)
-    parts = three_parts(mean_g + m2_g)
-    pad = jnp.zeros((half - 24, LANES), F32)
-    block = jnp.concatenate(list(parts) + [pad], axis=0).astype(BF16)
-    pay_ref[:, channels:] = block
+    hi, mid, lo = three_parts(mean_g + m2_g)
+    block = jnp.concatenate([hi + pltpu.roll(mid, 4, axis=0), lo], axis=0).astype(BF16)
+    top = pay_ref.shape[0] - 16
+    pay_ref[top:, :] = block
     st_ref[...] = block
     loads[2].wait()
     start = pl.multiple_of(lax.axis_index("sub") * half, half)
-    pay_ref[:, :channels] = thumb_ref[pl.ds(start, half), :]
+    for j in range(channels // LANES):
+        pay_ref[j * half : (j + 1) * half, :] = thumb_ref[pl.ds(start, half), j * LANES : (j + 1) * LANES]
 
 
 def meanwhile(thumb_ref, *refs):
@@ -104,46 +106,49 @@
         load.wait()
 
 
-def row_weights(ramps_ref, tile, n_tile, columns, upper):
-    owned = 2 * M
-    shape = (M * columns, 1)
-    row = lax.broadcasted_iota(jnp.int32, shape, 0)
+def row_weights(ramps_ref, tile, n_tile, columns, rows):
+    shape = (len(rows) * columns, 1)
+    place = lax.broadcasted_iota(jnp.int32, shape, 0)
     own = jnp.zeros(shape, F32)
     other = jnp.zeros(shape, F32)
-    if upper:
-        peer, live = jnp.maximum(tile - 1, 0), tile > 0
-    else:
-        peer, live = jnp.minimum(tile + 1, n_tile - 1), tile < n_tile - 1
-    gate = jnp.where(live, 1.0, 0.0).astype(F32)
-    for r in range(M):
-        here = (row >= r * columns) & (row < (r + 1) * columns)
-        own_r = ramps_ref[tile, (M if upper else 2 * M) + r].astype(F32)
-        other_r = ramps_ref[peer, (M + owned if upper else 0) + r].astype(F32) * gate
-        own = jnp.where(here, own_r, own)
+    for i, r in enumerate(rows):
+        here = (place >= i * columns) & (place < (i + 1) * columns)
+        if r < M:
+            peer, live, at = jnp.maximum(tile - 1, 0), tile > 0, 3 * M + r
+        else:
+            peer, live, at = jnp.minimum(tile + 1, n_tile - 1), tile < n_tile - 1, r - M
+        other_r = ramps_ref[peer, at].astype(F32) * jnp.where(live, 1.0, 0.0).astype(F32)
+        own = jnp.where(here, ramps_ref[tile, M + r].astype(F32), own)
         other = jnp.where(here, other_r, other)
     total = own + other
     return own / total, other / total
 
 
+def masked_keys(k, out_ref):
+    zero = jnp.zeros((k.shape[0], LANES), BF16)
+    low = lax.broadcasted_iota(jnp.int32, zero.shape, 1) < HD
+    for j in range(k.shape[1] // LANES):
+        pair = k[:, j * LANES : (j + 1) * LANES]
+        out_ref[:, 2 * j * LANES : (2 * j + 1) * LANES] = jnp.where(low, pair, zero)
+        out_ref[:, (2 * j + 1) * LANES : (2 * j + 2) * LANES] = jnp.where(low, zero, pair)
+
+
 def attend(q, k_ref, v_ref, wo_ref, weights, bl_ref, send_ref, own_ref, split):
     n = bl_ref.shape[0]
     w_own, w_other = weights
-    width = k_ref.shape[1]
+    width = v_ref.shape[1]
+    left = lax.broadcasted_iota(jnp.int32, (2 * n, LANES), 1) < HD
     for j in range(width // LANES):
         cols = slice(j * LANES, (j + 1) * LANES)
-        qp = q(cols)
-        kp, vp = k_ref[:, cols], v_ref[:, cols]
-        low = lax.broadcasted_iota(jnp.int32, kp.shape, 1) < HD
-        zero = jnp.zeros_like(kp)
-        out = None
+        qp, vp = q(cols), v_ref[:, cols]
+        outs = []
         for h in range(2):
-            keep = low if h == 0 else jnp.logical_not(low)
-            k_h, v_h = jnp.where(keep, kp, zero), jnp.where(keep, vp, zero)
+            k_h = k_ref[:, (2 * j + h) * LANES : (2 * j + h + 1) * LANES]
             s = lax.dot_general(qp, k_h, NT, preferred_element_type=F32)
             p = jnp.exp(s - jnp.max(s, axis=1, keepdims=True))
             total = jnp.sum(p, axis=1, keepdims=True)
-            o = jnp.dot(p.astype(BF16), v_h, preferred_element_type=F32) * (1.0 / total)
-            out = o if out is None else out + o
+            outs.append(jnp.dot(p.astype(BF16), vp, preferred_element_type=F32) * (1.0 / total))
+        out = jnp.where(left, outs[0], outs[1])
         att = out.astype(BF16).astype(F32)
         bl_ref[:, cols] = (att[:n] * w_own + att[n:] * w_other).astype(BF16)
     term = jnp.dot(bl_ref[...], wo_ref[...], preferred_element_type=F32)
@@ -185,19 +190,23 @@
     return gain, in_one_row(temb_ref, n, 2 * n)
 
 
-def fill_normed(canvas_ref, rows, affine, normed_ref, order):
+def fill_normed(canvas_ref, rows, columns, affine, normed_ref):
     chan, gain, shift = affine
-    n = normed_ref.shape[0] // 2
+    n = len(rows) * columns
+    upper = sum(r < M for r in rows) * columns
+    base = rows[0] * columns
+    runs = [(0, n, 0, 0), (0, upper, n, -1), (upper, n, n, 1)]
     for j in range(canvas_ref.shape[1] // LANES):
         cols = slice(j * LANES, (j + 1) * LANES)
-        x = canvas_ref[rows, cols].astype(F32)
-        for i, o in enumerate(order):
-            mean, rstd = chan[o + 1 : o + 2, cols], chan[o + 4 : o + 5, cols]
-            normed = (x - mean) * (rstd * gain[:, cols]) + shift[:, cols]
-            normed_ref[i * n : (i + 1) * n, cols] = normed.astype(BF16)
-
-
-def first_block(n_tile, split, count, columns, *refs):
+        for first, last, to, o in runs:
+            if last > first:
+                x = canvas_ref[base + first : base + last, cols].astype(F32)
+                mean, rstd = chan[o + 1 : o + 2, cols], chan[o + 4 : o + 5, cols]
+                normed = (x - mean) * (rstd * gain[:, cols]) + shift[:, cols]
+                normed_ref[to + first : to + last, cols] = normed.astype(BF16)
+
+
+def first_block(n_tile, split, count, columns, rows, *refs):
     (ramps_ref, canvas_ref, k_own_ref, v_own_ref, temb_ref, gain_ref, wq_ref, wk_ref, wv_ref, wo_ref) = refs[:10]
     st_ref, st_peer_ref = refs[10:12]
     near = refs[12 : 12 + n_tile - 1]
@@ -209,18 +218,17 @@
         send_ref, k_ref, v_ref, chan_ref, all_ref, normed_ref, q_ref, bl_ref = rest
         own_ref = None
     channels = canvas_ref.shape[1]
-    half = near[0].shape[0]
+    half = (near[0].shape[0] - 16) * LANES // channels
     tile = lax.axis_index("tile")
 
-    def stat(ref, lanes):
-        v = ref[:, lanes].astype(F32)
-        return v[0:8] + v[8:16] + v[16:24]
-
-    full, tail = slice(0, LANES), slice(channels, channels + LANES)
-    held = {0: [stat(st_ref, full), stat(st_peer_ref, full)]}
+    def stat(ref):
+        v = ref[ref.shape[0] - 16 :, :].astype(F32)
+        return v[0:8] + pltpu.roll(v[0:8], 4, axis=0) + v[8:16]
+
+    held = {0: [stat(st_ref), stat(st_peer_ref)]}
     for k in range(1, n_tile):
         if in_pairs(n_tile) or min(k, n_tile - k) <= 2:
-            held[k] = [stat(near[k - 1], tail), stat(far[k - 1], tail)]
+            held[k] = [stat(near[k - 1]), stat(far[k - 1])]
     stats = {}
     for o in range(-2, 3):
         stats[o] = [jnp.zeros_like(v) for v in held[0]]
@@ -229,22 +237,23 @@
             stats[o] = [a + v * hit for a, v in zip(stats[o], got)]
     chan = merged_stats(stats, float(count), group_of_channel(channels))
     gain, shift = gain_and_shift(temb_ref, gain_ref)
-    n = normed_ref.shape[0] // 2
-    fill_normed(canvas_ref, slice(0, n), (chan, gain, shift), normed_ref, (0, -1))
+    fill_normed(canvas_ref, rows, columns, (chan, gain, shift), normed_ref)
     chan_ref[...] = chan
     q_ref[...] = (jnp.dot(normed_ref[...], wq_ref[...], preferred_element_type=F32).astype(BF16)) * 0.125
 
     own_rows = k_own_ref.shape[0]
     for i, ref in enumerate(near + far):
-        all_ref[i * half : (i + 1) * half, :] = ref[:, :channels]
-    k_ref[:own_rows, :], v_ref[:own_rows, :] = k_own_ref[...], v_own_ref[...]
-    k_ref[own_rows:, :] = jnp.dot(all_ref[...], wk_ref[...], preferred_element_type=F32).astype(BF16)
+        for j in range(channels // LANES):
+            all_ref[i * half : (i + 1) * half, j * LANES : (j + 1) * LANES] = ref[j * half : (j + 1) * half, :]
+    v_ref[:own_rows, :] = v_own_ref[...]
+    masked_keys(k_own_ref[...], k_ref.at[:own_rows, :])
+    masked_keys(jnp.dot(all_ref[...], wk_ref[...], preferred_element_type=F32).astype(BF16), k_ref.at[own_rows:, :])
     v_ref[own_rows:, :] = jnp.dot(all_ref[...], wv_ref[...], preferred_element_type=F32).astype(BF16)
-    weights = row_weights(ramps_ref, tile, n_tile, columns, True)
+    weights = row_weights(ramps_ref, tile, n_tile, columns, rows)
     attend(lambda cols: q_ref[:, cols], k_ref, v_ref, wo_ref, weights, bl_ref, send_ref, own_ref, split)
 
 
-def second_block(n_tile, split, columns, *refs):
+def next_block(n_tile, split, columns, rows, *refs):
     ramps_ref, canvas_ref, temb_ref, gain_ref, wq_ref, wo_ref, k_ref, v_ref, chan_ref = refs[:9]
     if split:
         send_ref, own_ref, normed_ref, q_ref, bl_ref = refs[9:]
@@ -253,17 +262,21 @@
         own_ref = None
     tile = lax.axis_index("tile")
     gain, shift = gain_and_shift(temb_ref, gain_ref)
-    n = normed_ref.shape[0] // 2
-    fill_normed(canvas_ref, slice(n, 2 * n), (chan_ref[...], gain, shift), normed_ref, (0, 1))
+    fill_normed(canvas_ref, rows, columns, (chan_ref[...], gain, shift), normed_ref)
     q_ref[...] = (jnp.dot(normed_ref[...], wq_ref[...], preferred_element_type=F32).astype(BF16)) * 0.125
-    weights = row_weights(ramps_ref, tile, n_tile, columns, False)
+    weights = row_weights(ramps_ref, tile, n_tile, columns, rows)
     attend(lambda cols: q_ref[:, cols], k_ref, v_ref, wo_ref, weights, bl_ref, send_ref, own_ref, split)
 
 
-def add_up(own_a, got_a, own_b, got_b, out_ref):
-    n = own_a.shape[0]
-    out_ref[:n, :] = (own_a[...].astype(F32) + got_a[...].astype(F32)).astype(BF16)
-    out_ref[n:, :] = (own_b[...].astype(F32) + got_b[...].astype(F32)).astype(BF16)
+def add_up(places, *refs):
+    out_ref, sum_ref, sem = refs[-3:]
+    base, length = places[0][0], sum(n for _, n in places)
+    for i, (first, n) in enumerate(places):
+        total = refs[2 * i][...].astype(F32) + refs[2 * i + 1][...].astype(F32)
+        sum_ref[first - base : first - base + n, :] = total.astype(BF16)
+    write = pltpu.make_async_copy(sum_ref, out_ref.at[pl.ds(base, length)], sem)
+    write.start()
+    write.wait()
 
 
 def resident(*arrays):
@@ -297,9 +310,9 @@
         grow = width - local_ch
         w_query, w_key, w_value = (jnp.pad(w, ((0, 0), (0, grow))) for w in (w_query, w_key, w_value))
         w_out = jnp.pad(w_out, ((0, grow), (0, 0)))
-    rows = owned * columns
-    n = rows // 2
-    x = canvas.reshape(rows, channels)
+    rows_all = owned * columns
+    n = rows_all // 2
+    x = canvas.reshape(rows_all, channels)
     half = thumb.shape[0] // n_sub
     tokens = thumb.shape[0] * n_tile
     count = n * (channels // GROUPS)
@@ -311,8 +324,8 @@
     payload, st, x, thumb = pl.pallas_call(
         local_stats,
         out_shape=(
-            pltpu.VMEM((half, channels + LANES), BF16),
-            pltpu.VMEM((half, LANES), BF16),
+            pltpu.VMEM((half * channels // LANES + 16, LANES), BF16),
+            pltpu.VMEM((16, LANES), BF16),
             pltpu.VMEM(x.shape, BF16),
             pltpu.VMEM(thumb.shape, BF16),
         ),
@@ -348,51 +361,71 @@
     st_peer = shifted(st, "sub", 1)
     far = [shifted(v, "sub", 1) for v in near]
 
-    part = pltpu.VMEM((n, channels // 2 if split else channels), BF16)
-    parts = (part, part) if split else (part,)
-    work = [
-        pltpu.VMEM((2 * n, channels), BF16),
-        pltpu.VMEM((2 * n, width), BF16),
-        pltpu.VMEM((n, width), BF16),
-    ]
+    blocks, places, first_row = [], [], 0
+    for size in CHUNKS:
+        blocks.append(tuple(range(first_row, first_row + size)))
+        places.append((first_row * columns, size * columns))
+        first_row += size
+
+    def results(rows):
+        part = pltpu.VMEM((len(rows) * columns, channels // 2 if split else channels), BF16)
+        return (part, part) if split else (part,)
+
+    def work(rows):
+        size = len(rows) * columns
+        return [pltpu.VMEM((2 * size, channels), BF16), pltpu.VMEM((2 * size, width), BF16), pltpu.VMEM((size, width), BF16)]
+
     kv = pltpu.VMEM((tokens, width), BF16)
+    parts = results(blocks[0])
     outs = pl.pallas_call(
-        functools.partial(first_block, n_tile, split, count, columns),
-        out_shape=parts + (kv, kv, pltpu.VMEM((8, channels), F32)),
+        functools.partial(first_block, n_tile, split, count, columns, blocks[0]),
+        out_shape=parts + (pltpu.VMEM((tokens, 2 * width), BF16), kv, pltpu.VMEM((8, channels), F32)),
         in_specs=[smem] + [vmem] * (11 + 2 * (n_tile - 1)),
         out_specs=(vmem,) * (len(parts) + 3),
-        scratch_shapes=[pltpu.VMEM((tokens - thumb.shape[0], channels), BF16)] + work,
+        scratch_shapes=[pltpu.VMEM((tokens - thumb.shape[0], channels), BF16)] + work(blocks[0]),
         compiler_params=pltpu.CompilerParams(vmem_limit_bytes=24 << 20),
         name="first_block",
     )(
         *(ramps, x, k_own, v_own, temb, gain, w_query, w_key, w_value, w_out),
         *resident(st, st_peer, *near, *far),
     )
-    first, (keys, values, chan) = outs[: len(parts)], outs[len(parts) :]
-    got_a = shifted(first[0], "chan", 1) if split else None
-    more = pl.pallas_call(
-        functools.partial(second_block, n_tile, split, columns),
-        out_shape=parts,
-        in_specs=[smem] + [vmem] * 8,
-        out_specs=(vmem,) * len(parts),
-        scratch_shapes=work,
-        compiler_params=pltpu.CompilerParams(vmem_limit_bytes=20 << 20),
-        name="second_block",
-    )
-    second = more(ramps, x, temb, gain, w_query, w_out, *resident(keys, values, chan))
-    if split:
-        got_b = shifted(second[0], "chan", 1)
-        out = pl.pallas_call(
-            add_up,
-            out_shape=jax.ShapeDtypeStruct((rows, channels // 2), BF16),
-            in_specs=[vmem] * 4,
-            out_specs=vmem,
+    kept = resident(*outs[len(parts) :])
+    done = [outs[: len(parts)]]
+    got = [shifted(done[0][0], "chan", 1)] if split else []
+    for i, rows in enumerate(blocks[1:], 1):
+        block = pl.pallas_call(
+            functools.partial(next_block, n_tile, split, columns, rows),
+            out_shape=results(rows),
+            in_specs=[smem] + [vmem] * 8,
+            out_specs=(vmem,) * len(parts),
+            scratch_shapes=work(rows),
+            compiler_params=pltpu.CompilerParams(vmem_limit_bytes=20 << 20),
+        )
+        done.append(block(ramps, x, temb, gain, w_query, w_out, *kept))
+        if split:
+            got.append(shifted(done[i][0], "chan", 1))
+    if not split:
+        both = jnp.concatenate([d[0] for d in done], axis=0)
+        out = lax.psum_scatter(both, "chan", scatter_dimension=1, tiled=True)
+        return out.reshape(owned, columns, out.shape[1])
+
+    def added(span, into):
+        pairs = [v for i in span for v in (done[i][1], got[i])]
+        length = sum(places[i][1] for i in span)
+        earlier = [] if into is None else in_hbm(into)
+        return pl.pallas_call(
+            functools.partial(add_up, tuple(places[i] for i in span)),
+            out_shape=jax.ShapeDtypeStruct((rows_all, channels // 2), BF16),
+            in_specs=[vmem] * len(pairs) + [hbm] * len(earlier),
+            out_specs=hbm,
+            scratch_shapes=[pltpu.VMEM((length, channels // 2), BF16), pltpu.SemaphoreType.DMA],
+            input_output_aliases={len(pairs): 0} if earlier else {},
             compiler_params=pltpu.CompilerParams(vmem_limit_bytes=4 << 20),
-        name="add_up",
-        )(*resident(first[1], got_a, second[1], got_b))
-    else:
-        both = jnp.concatenate([first[0], second[0]], axis=0)
-        out = lax.psum_scatter(both, "chan", scatter_dimension=1, tiled=True)
+        )(*resident(*pairs), *earlier)
+
+    last = len(blocks) - 1
+    out = added(range(last), None)
+    out = added(range(last, last + 1), out)
     return out.reshape(owned, columns, out.shape[1])
 
 

time: 33.2 us -> 32.7 us (0.985)
  waiting for transfers between devices: 12.7 us -> 11.6 us
  Pallas kernels: 11.8 us -> 12.4 us
    ppermute x9, waiting for transfers between devices: 12.7 us -> 11.6 us  [shifted(): lax.ppermute(value, axis, [(partner(i, count, step), i) for i in range(co...]
    pallas_call x3 -> x4, Pallas kernels: 5.17 us -> 5.75 us  [the longest x1 2.58 us: on_device(): done.append(block(ramps, x, temb, gain, w_query, w_out, *kept))]
  transfers between devices with their start and end apart: 9 -> 9, of which waited for: 4 -> 4; matrix products, arithmetic and copies ran while one was open for 0% -> 0% of each run, Pallas kernels for 17% -> 19%
where the time goes in v4:
time: 32.7 us; the launch traced here: 32.6 us
  Pallas kernels  12.4 us (38%)
  waiting for transfers between devices  11.6 us (35%)
  starting transfers between devices  8.46 us (26%)
    ppermute x9, waiting for transfers between devices, shifted(): lax.ppermute(value, axis, [(partner(i, count, step), i) for i in range(co...  11.6 us
    ppermute x9, starting transfers between devices, shifted(): lax.ppermute(value, axis, [(partner(i, count, step), i) for i in range(co...  8.46 us
    pallas_call x1, Pallas kernels, on_device(): pl.pallas_call(functools.partial(first_block, n_tile, split, count, colum...  3.64 us
    pallas_call x1, Pallas kernels, on_device(): *brought, k_own, v_own = bring(thumb, *in_hbm(*brought))  2.98 us
    pallas_call x1, Pallas kernels, on_device(): done.append(block(ramps, x, temb, gain, w_query, w_out, *kept))  2.58 us
    pallas_call x1, Pallas kernels, on_device(): pl.pallas_call(local_stats, out_shape=(pltpu.VMEM((half * channels // LAN...  1.73 us
    pallas_call x2, Pallas kernels, added(): pl.pallas_call(functools.partial(add_up, tuple((places[i] for i in span))...  1.43 us
  transfers between devices with their start and end apart: 9, of which 4 were waited for; matrix products, arithmetic and copies ran while one was open for 0% of the time, Pallas kernels for 19%

profile of v4, /device:TPU:0, one launch (start us, length us, event | category | flops | bytes accessed | tf_op | source)
XLA Modules:
  0.0 32.6 jit_solution(9620716926793156303)
XLA Ops:
  0.0 1.7 %local_stats.1 = (bf16[336,128]{1,0:T(8,128)(2,1)S(1)}, bf16[16,128]{1,0:T(8,128)(2,1)S(1)}, bf16[256,1280]{1,0:T(8,128)(2,1)S(1)}, bf16[64,1280]{1,0:T(8,128)(2,1)S(1)}) custom-call(bf16[256,1280]{1,0:T(8,128)(2,1)} %bitcast.4, bf16[64,1280]{1,0:T(8,128)(2,1)} %thumb_hbm.1), custom_call_target="tpu_custom_call" | custom-call | tf_op jit(solution)/shard_map/local_stats/pallas_call | solution.py:324
  1.7 5.1 %collective-permute-start.3 = (bf16[336,128]{1,0:T(8,128)(2,1)S(1)}, bf16[336,128]{1,0:T(8,128)(2,1)S(1)}, u32[]{:S(2)}, u32[]{:S(2)}) collective-permute-start(bf16[336,128]{1,0:T(8,128)(2,1)S(1)} %get-tuple-element.35), channel_id=1, source_target_pairs={{12,0},{8,4},{4,8},{0,12},{13,1},{9,5},{5,9},{1,13},{14,2},{10,6},... | collective-permute-start | bytes 258056 | tf_op jit(solution)/shard_map/ppermute | solution.py:292
  6.9 0.0 collective-permute-start.2
  6.9 0.6 %collective-permute-start.1 = (bf16[336,128]{1,0:T(8,128)(2,1)S(1)}, bf16[336,128]{1,0:T(8,128)(2,1)S(1)}, u32[]{:S(2)}, u32[]{:S(2)}) collective-permute-start(bf16[336,128]{1,0:T(8,128)(2,1)S(1)} %get-tuple-element.35), channel_id=1, source_target_pairs={{4,0},{0,4},{12,8},{8,12},{5,1},{1,5},{13,9},{9,13},{6,2},{2,6},{1... | collective-permute-start | bytes 258056 | tf_op jit(solution)/shard_map/ppermute | solution.py:292
  7.5 2.5 %collective-permute-done.3.refs_14_ = bf16[336,128]{1,0:T(8,128)(2,1)S(1)} collective-permute-done((bf16[336,128]{1,0:T(8,128)(2,1)S(1)}, bf16[336,128]{1,0:T(8,128)(2,1)S(1)}, u32[]{:S(2)}, u32[]{:S(2)}) %collective-permute-start.3) | collective-permute-done | bytes 86048 | tf_op jit(solution)/shard_map/ppermute | solution.py:292
  10.0 0.0 collective-permute-start.6
  10.0 4.0 %collective-permute-done.2.refs_13_ = bf16[336,128]{1,0:T(8,128)(2,1)S(1)} collective-permute-done((bf16[336,128]{1,0:T(8,128)(2,1)S(1)}, bf16[336,128]{1,0:T(8,128)(2,1)S(1)}, u32[]{:S(2)}, u32[]{:S(2)}) %collective-permute-start.2) | collective-permute-done | bytes 86048 | tf_op jit(solution)/shard_map/ppermute | solution.py:292
  14.1 0.0 collective-permute-start.5
  14.1 0.0 collective-permute-done.1.refs_12_
  14.1 0.5 %collective-permute-start.4 = (bf16[336,128]{1,0:T(8,128)(2,1)S(1)}, bf16[336,128]{1,0:T(8,128)(2,1)S(1)}, u32[]{:S(2)}, u32[]{:S(2)}) collective-permute-start(bf16[336,128]{1,0:T(8,128)(2,1)S(1)} %collective-permute-done.1.refs_12_), channel_id=1, source_target_pairs={{1,0},{0,1},{3,2},{2,3},{5,4},{4,5},{7,6},{6,7},{9,8},{8,9},{11,10... | collective-permute-start | bytes 258056 | tf_op jit(solution)/shard_map/ppermute | solution.py:292
  14.6 0.0 collective-permute-start
  14.6 0.0 copy-start
  14.6 3.0 %meanwhile.1 = (bf16[1280,640]{1,0:T(8,128)(2,1)S(1)}, bf16[1280,640]{1,0:T(8,128)(2,1)S(1)}, bf16[1280,640]{1,0:T(8,128)(2,1)S(1)}, bf16[640,1280]{1,0:T(8,128)...) custom-call(bf16[64,1280]{1,0:T(8,128)(2,1)S(1)} %get-tuple-element., ...), custom_call_target="tpu_custom_call" | custom-call | tf_op jit(solution)/shard_map/meanwhile/pallas_call | solution.py:352
  17.6 0.0 collective-permute-done.refs_11_
  17.6 0.0 collective-permute-done.6.refs_17_
  17.6 0.0 collective-permute-done.5.refs_16_
  17.6 0.0 collective-permute-done.4.refs_15_
  17.6 0.0 copy-done
  17.7 3.6 %first_block.1 = (bf16[128,640]{1,0:T(8,128)(2,1)S(1)}, bf16[128,640]{1,0:T(8,128)(2,1)S(1)}, bf16[256,1280]{1,0:T(8,128)(2,1)S(1)}, bf16[256,640]{1,0:T(8,128)(2,1)S(1)}, f32[8,1280]{1,0:T(8,128)S(1)}) custom-call(s32[4,16]{1,0:T(4,128)S(1)} %copy-done, bf16[256,1280]{1,0:T(8,128)(2,1)S(1)} %get-tuple-element.24.refs_1_, ...), custom_call_target="tpu_custom_call" | custom-call | tf_op jit(solution)/shard_map/first_block/pallas_call | solution.py:380
  21.3 1.6 %collective-permute-start.8 = (bf16[128,640]{1,0:T(8,128)(2,1)S(1)}, bf16[128,640]{1,0:T(8,128)(2,1)S(1)}, u32[]{:S(2)}, u32[]{:S(2)}) collective-permute-start(bf16[128,640]{1,0:T(8,128)(2,1)S(1)} %get-tuple-element.42), channel_id=1, source_target_pairs={{2,0},{0,2},{3,1},{1,3},{6,4},{4,6},{7,5},{5,7},{10,8},{8,10},{11,... | collective-permute-start | bytes 491528 | tf_op jit(solution)/shard_map/ppermute | solution.py:292
  22.9 2.6 %shard_map.91 = (bf16[128,640]{1,0:T(8,128)(2,1)S(1)}, bf16[128,640]{1,0:T(8,128)(2,1)S(1)}) custom-call(s32[4,16]{1,0:T(4,128)S(1)} %copy-done, bf16[256,1280]{1,0:T(8,128)(2,1)S(1)} %get-tuple-element.24.refs_1_, f32[20,128]{1,0:T(8,128)S(1)} %get-tuple-element.26.refs_4_.refs_2_, f32[10,128]{1,0:T(8,128)S(1)} %get-tuple-element.27.refs_5_.refs_3_, ...), custom_call_target="tpu_custom_call" | custom-call | tf_op jit(solution)/shard_map/pallas_call | solution.py:404
  25.5 0.6 %collective-permute-start.7 = (bf16[128,640]{1,0:T(8,128)(2,1)S(1)}, bf16[128,640]{1,0:T(8,128)(2,1)S(1)}, u32[]{:S(2)}, u32[]{:S(2)}) collective-permute-start(bf16[128,640]{1,0:T(8,128)(2,1)S(1)} %get-tuple-element.40), channel_id=1, source_target_pairs={{2,0},{0,2},{3,1},{1,3},{6,4},{4,6},{7,5},{5,7},{10,8},{8,10},{11,... | collective-permute-start | bytes 491528 | tf_op jit(solution)/shard_map/ppermute | solution.py:292
  26.1 1.9 %collective-permute-done.8.refs_1_ = bf16[128,640]{1,0:T(8,128)(2,1)S(1)} collective-permute-done((bf16[128,640]{1,0:T(8,128)(2,1)S(1)}, bf16[128,640]{1,0:T(8,128)(2,1)S(1)}, u32[]{:S(2)}, u32[]{:S(2)}) %collective-permute-start.8) | collective-permute-done | bytes 163872 | tf_op jit(solution)/shard_map/ppermute | solution.py:292
  28.0 0.7 %shard_map.92.refs_2_ = bf16[256,640]{1,0:T(8,128)(2,1)} custom-call(bf16[128,640]{1,0:T(8,128)(2,1)S(1)} %get-tuple-element.41.refs_0_, bf16[128,640]{1,0:T(8,128)(2,1)S(1)} %collective-permute-done.8.refs_1_), custom_call_target="tpu_custom_call" | custom-call | tf_op jit(solution)/shard_map/pallas_call | solution.py:416
  28.7 3.1 %collective-permute-done.7.refs_1_ = bf16[128,640]{1,0:T(8,128)(2,1)S(1)} collective-permute-done((bf16[128,640]{1,0:T(8,128)(2,1)S(1)}, bf16[128,640]{1,0:T(8,128)(2,1)S(1)}, u32[]{:S(2)}, u32[]{:S(2)}) %collective-permute-start.7) | collective-permute-done | bytes 163872 | tf_op jit(solution)/shard_map/ppermute | solution.py:292
  31.8 0.7 %shard_map.93 = bf16[256,640]{1,0:T(8,128)(2,1)} custom-call(bf16[128,640]{1,0:T(8,128)(2,1)S(1)} %get-tuple-element.39.refs_0_, bf16[128,640]{1,0:T(8,128)(2,1)S(1)} %collective-permute-done.7.refs_1_, bf16[256,640]{1,0:T(8,128)(2,1)} %shard_map.92.refs_2_), custom_call_target="tpu_custom_call", output_to_operand_aliasing={{}: (2, {})} | custom-call | tf_op jit(solution)/shard_map/pallas_call | solution.py:416
Async XLA Ops:
  1.7 8.3 %collective-permute-start.3 = (bf16[336,128]{1,0:T(8,128)(2,1)S(1)}, bf16[336,128]{1,0:T(8,128)(2,1)S(1)}, u32[]{:S(2)}, u32[]{:S(2)}) collective-permute-start(bf16[336,128]{1,0:T(8,128)(2,1)S(1)} %get-tuple-element.35), channel_id=1, source_target_pairs={{12,0},{8,4},{4,8},{0,12},{13,1},{9,5},{5,9},{1,13},{14,2},{10,6},... | collective-permute-start | bytes 258056 | tf_op jit(solution)/shard_map/ppermute | solution.py:292
  6.9 7.2 %collective-permute-start.2 = (bf16[336,128]{1,0:T(8,128)(2,1)S(1)}, bf16[336,128]{1,0:T(8,128)(2,1)S(1)}, u32[]{:S(2)}, u32[]{:S(2)}) collective-permute-start(bf16[336,128]{1,0:T(8,128)(2,1)S(1)} %get-tuple-element.35), channel_id=1, source_target_pairs={{8,0},{12,4},{0,8},{4,12},{9,1},{13,5},{1,9},{5,13},{10,2},{14,6},... | collective-permute-start | bytes 258056 | tf_op jit(solution)/shard_map/ppermute | solution.py:292
  6.9 7.2 %collective-permute-start.1 = (bf16[336,128]{1,0:T(8,128)(2,1)S(1)}, bf16[336,128]{1,0:T(8,128)(2,1)S(1)}, u32[]{:S(2)}, u32[]{:S(2)}) collective-permute-start(bf16[336,128]{1,0:T(8,128)(2,1)S(1)} %get-tuple-element.35), channel_id=1, source_target_pairs={{4,0},{0,4},{12,8},{8,12},{5,1},{1,5},{13,9},{9,13},{6,2},{2,6},{1... | collective-permute-start | bytes 258056 | tf_op jit(solution)/shard_map/ppermute | solution.py:292
  10.0 7.6 %collective-permute-start.6 = (bf16[336,128]{1,0:T(8,128)(2,1)S(1)}, bf16[336,128]{1,0:T(8,128)(2,1)S(1)}, u32[]{:S(2)}, u32[]{:S(2)}) collective-permute-start(bf16[336,128]{1,0:T(8,128)(2,1)S(1)} %collective-permute-done.3.refs_14_), channel_id=1, source_target_pairs={{1,0},{0,1},{3,2},{2,3},{5,4},{4,5},{7,6},{6,7},{9,8},{8,9},{11,10... | collective-permute-start | bytes 258056 | tf_op jit(solution)/shard_map/ppermute | solution.py:292
  14.1 3.5 %collective-permute-start.5 = (bf16[336,128]{1,0:T(8,128)(2,1)S(1)}, bf16[336,128]{1,0:T(8,128)(2,1)S(1)}, u32[]{:S(2)}, u32[]{:S(2)}) collective-permute-start(bf16[336,128]{1,0:T(8,128)(2,1)S(1)} %collective-permute-done.2.refs_13_), channel_id=1, source_target_pairs={{1,0},{0,1},{3,2},{2,3},{5,4},{4,5},{7,6},{6,7},{9,8},{8,9},{11,10... | collective-permute-start | bytes 258056 | tf_op jit(solution)/shard_map/ppermute | solution.py:292
  14.1 3.5 %collective-permute-start.4 = (bf16[336,128]{1,0:T(8,128)(2,1)S(1)}, bf16[336,128]{1,0:T(8,128)(2,1)S(1)}, u32[]{:S(2)}, u32[]{:S(2)}) collective-permute-start(bf16[336,128]{1,0:T(8,128)(2,1)S(1)} %collective-permute-done.1.refs_12_), channel_id=1, source_target_pairs={{1,0},{0,1},{3,2},{2,3},{5,4},{4,5},{7,6},{6,7},{9,8},{8,9},{11,10... | collective-permute-start | bytes 258056 | tf_op jit(solution)/shard_map/ppermute | solution.py:292
  14.6 3.0 %collective-permute-start = (bf16[16,128]{1,0:T(8,128)(2,1)S(1)}, bf16[16,128]{1,0:T(8,128)(2,1)S(1)}, u32[]{:S(2)}, u32[]{:S(2)}) collective-permute-start(bf16[16,128]{1,0:T(8,128)(2,1)S(1)} %get-tuple-element.34.refs_10_), channel_id=1, source_target_pairs={{1,0},{0,1},{3,2},{2,3},{5,4},{4,5},{7,6},{6,7},{9,8},{8,9},{11,10... | collective-permute-start | bytes 12296 | tf_op jit(solution)/shard_map/ppermute | solution.py:292
  14.6 3.0 %copy-start = (s32[4,16]{1,0:T(4,128)S(1)}, s32[4,16]{1,0:T(4,128)}, u32[]{:S(2)}) copy-start(s32[4,16]{1,0:T(4,128)} %refs_0_.5) | copy-start | bytes 772
  21.3 6.7 %collective-permute-start.8 = (bf16[128,640]{1,0:T(8,128)(2,1)S(1)}, bf16[128,640]{1,0:T(8,128)(2,1)S(1)}, u32[]{:S(2)}, u32[]{:S(2)}) collective-permute-start(bf16[128,640]{1,0:T(8,128)(2,1)S(1)} %get-tuple-element.42), channel_id=1, source_target_pairs={{2,0},{0,2},{3,1},{1,3},{6,4},{4,6},{7,5},{5,7},{10,8},{8,10},{11,... | collective-permute-start | bytes 491528 | tf_op jit(solution)/shard_map/ppermute | solution.py:292
  25.5 6.4 %collective-permute-start.7 = (bf16[128,640]{1,0:T(8,128)(2,1)S(1)}, bf16[128,640]{1,0:T(8,128)(2,1)S(1)}, u32[]{:S(2)}, u32[]{:S(2)}) collective-permute-start(bf16[128,640]{1,0:T(8,128)(2,1)S(1)} %get-tuple-element.40), channel_id=1, source_target_pairs={{2,0},{0,2},{3,1},{1,3},{6,4},{4,6},{7,5},{5,7},{10,8},{8,10},{11,... | collective-permute-start | bytes 491528 | tf_op jit(solution)/shard_map/ppermute | solution.py:292
